TPU v7x, 256 devices: a whole 4x4x8 slice. The times are simulated.
256 devices in a mesh: species: 16 (over y, z_lo, core), tile: 16 (over x, z_hi).
Axes of the slice: x: 4, y: 4, z: 8 (z_hi: 4, z_lo: 2; z = z_hi * 2 + z_lo), core: 2. Of those that a mesh axis runs over, the one named last changes fastest.
Arguments:
- tracers: float32 [256, 16, 128, 128], P('species', None, 'tile'), may hold values from 0.1 to 4
- fluxes: float32 [4, 3, 16, 128, 128], P(None, None, 'species', 'tile'), may hold values from -0.15 to 0.15
- weight_in: bfloat16 [512, 256], replicated, may hold values from -0.375 to 0.375
- weight_out: bfloat16 [256, 512], replicated, may hold values from -0.25 to 0.25
Outputs:
- tracers_out: float32 [256, 16, 128, 128], P('species', None, 'tile')
All inputs are finite; a program needn't handle non-finite values.
Results may differ from a plain program's by a relative error of at most 0.0035.
Values may be sent and summed in bfloat16 or wider, within the bound.
A program may use at most 64 MiB of HBM per device.

v0:
```python
import jax
import jax.numpy as jnp
from jax import lax
from jax.sharding import PartitionSpec as P

STEPS = 4


def extended(cells, sides, width):
    for axis, dim in sides:
        count = lax.axis_size(axis)
        ends = count - 1
        head = lax.slice_in_dim(cells, 0, width, axis=dim)
        tail = lax.slice_in_dim(cells, cells.shape[dim] - width, cells.shape[dim], axis=dim)
        cells = jnp.concatenate(
            [
                lax.ppermute(tail, axis, [(i, (i + 1) % count) for i in range(ends)]),
                cells,
                lax.ppermute(head, axis, [((i + 1) % count, i) for i in range(ends)]),
            ],
            axis=dim,
        )
    return cells


def positive(value):
    return jnp.maximum(value, 0.0)


def negative(value):
    return jnp.minimum(value, 0.0)


def advance(padded_state, padded_x, flux_y, padded_z):
    inner = padded_state[:, 1:-1, 1:-1]
    along_x = padded_state[:, 1:-1]
    face_x = padded_x[:, 1:]
    faces_x = positive(face_x) * along_x[:, :, :-1] + negative(face_x) * along_x[:, :, 1:]
    along_z = padded_state[:, :, 1:-1]
    face_z = padded_z[1:]
    faces_z = positive(face_z) * along_z[:, :-1] + negative(face_z) * along_z[:, 1:]
    faces_y = positive(flux_y) * jnp.roll(inner, 1, 3) + negative(flux_y) * inner
    return (
        inner
        + faces_x[:, :, :-1]
        - faces_x[:, :, 1:]
        + faces_y
        - jnp.roll(faces_y, -1, 3)
        + faces_z[:, :-1]
        - faces_z[:, 1:]
    )


def per_device(tracers, fluxes, weight_in, weight_out):
    spec_loc, depth_all, width_x, width_y = tracers.shape
    tile_at = lax.axis_index("tile")
    grid_shape = (depth_all, width_x, width_y)
    column = tile_at * width_x + lax.broadcasted_iota(jnp.int32, grid_shape, 1)
    level_at = lax.broadcasted_iota(jnp.int32, grid_shape, 0)
    state = tracers
    for interval in range(STEPS):
        gathered = lax.all_gather(fluxes[interval], "species", axis=1, tiled=True)
        flux_x = jnp.where(column == 0, 0.0, gathered[0])
        flux_y = gathered[1]
        flux_z = jnp.where(level_at == 0, 0.0, gathered[2])
        stacked = jnp.concatenate([state, flux_x[None]], 0)
        padded = extended(stacked, (("tile", 2),), 1)
        padded_state = jnp.pad(padded[:spec_loc], ((0, 0), (1, 1), (0, 0), (0, 0)))
        padded_x = padded[spec_loc]
        padded_z = jnp.pad(flux_z, ((1, 1), (0, 0), (0, 0)))
        state = advance(padded_state, padded_x, flux_y, padded_z)
        flattened = state.astype(jnp.bfloat16).reshape(spec_loc, depth_all, width_x * width_y)
        hidden = jax.nn.silu(
            jnp.einsum(
                "hs,szc->hzc",
                weight_in,
                lax.all_to_all(flattened, "species", split_axis=1, concat_axis=0, tiled=True),
                preferred_element_type=jnp.float32,
            )
        ).astype(jnp.bfloat16)
        tendency = (
            0.5 * jnp.einsum("sh,hzc->szc", weight_out, hidden, preferred_element_type=jnp.float32)
        ).astype(jnp.bfloat16)
        returned = lax.all_to_all(tendency, "species", split_axis=0, concat_axis=1, tiled=True)
        state = state + returned.reshape(state.shape).astype(jnp.float32)
    return state


def solution(mesh):
    placed = (P("species", None, "tile", None), P(None, None, "species", "tile", None), P(), P())
    return jax.shard_map(
        per_device,
        mesh=mesh,
        in_specs=placed,
        out_specs=P("species", None, "tile", None),
        check_vma=False,
    )
```

profile of v0, /device:TPU:2, one launch (start us, length us, event | category | flops | bytes accessed | tf_op | source)
XLA Modules:
  0.0 284.3 jit_solution(3213758071041824670)
XLA Ops:
  0.9 21.1 %all-gather = f32[1,3,16,8,128]{4,3,1,0,2:T(8,128)S(1)} all-gather(f32[1,3,1,8,128]{4,3,1,0,2:T(8,128)S(1)} %get-tuple-element.47), channel_id=2, replica_groups=mesh['species'=16,'tile'=16] {'species'}, dimensions={2}, use_global_device_ids=true | all-gather | bytes 208896 | tf_op jit(solution)/shard_map/all_gather | solution.py:62
  21.9 17.0 %all-gather.1 = f32[1,3,16,8,128]{4,3,1,0,2:T(8,128)S(1)} all-gather(f32[1,3,1,8,128]{4,3,1,0,2:T(8,128)S(1)} %get-tuple-element.50), channel_id=3, replica_groups=mesh['species'=16,'tile'=16] {'species'}, dimensions={2}, use_global_device_ids=true | all-gather | bytes 208896 | tf_op jit(solution)/shard_map/all_gather | solution.py:62
  39.0 18.4 %all-gather.2 = f32[1,3,16,8,128]{4,3,1,0,2:T(8,128)S(1)} all-gather(f32[1,3,1,8,128]{4,3,1,0,2:T(8,128)S(1)} %get-tuple-element.49), channel_id=4, replica_groups=mesh['species'=16,'tile'=16] {'species'}, dimensions={2}, use_global_device_ids=true | all-gather | bytes 208896 | tf_op jit(solution)/shard_map/all_gather | solution.py:62
  57.3 17.0 %all-gather.3 = f32[1,3,16,8,128]{4,3,1,0,2:T(8,128)S(1)} all-gather(f32[1,3,1,8,128]{4,3,1,0,2:T(8,128)S(1)} %get-tuple-element.48), channel_id=5, replica_groups=mesh['species'=16,'tile'=16] {'species'}, dimensions={2}, use_global_device_ids=true | all-gather | bytes 208896 | tf_op jit(solution)/shard_map/all_gather | solution.py:62
  77.8 7.3 %collective-permute-start.1 = (f32[17,16,1,128]{3,1,2,0:T(8,128)S(1)}, f32[17,16,1,128]{3,1,2,0:T(8,128)S(1)}, u32[]{:S(2)}, u32[]{:S(2)}) collective-permute-start(f32[17,16,1,128]{3,1,2,0:T(8,128)S(1)} %get-tuple-element.20), channel_id=1, source_target_pairs={{1,0},{2,1},{3,2},{4,3},{5,4},{6,5},{7,6},{8,7},{9,8},{10,9},{11,1... | collective-permute-start | bytes 417800 | tf_op jit(solution)/shard_map/ppermute | solution.py:19
  90.3 8.3 %collective-permute-done = f32[17,16,1,128]{3,1,2,0:T(8,128)S(1)} collective-permute-done((f32[17,16,1,128]{3,1,2,0:T(8,128)S(1)}, f32[17,16,1,128]{3,1,2,0:T(8,128)S(1)}, u32[]{:S(2)}, u32[]{:S(2)}) %collective-permute-start) | collective-permute-done | bytes 139296 | tf_op jit(solution)/shard_map/ppermute | solution.py:17
  100.5 13.5 %all_to_all.96 = bf16[16,16,1024]{2,0,1:T(8,128)(2,1)S(1)} all-to-all(bf16[16,16,1024]{2,0,1:T(8,128)(2,1)S(1)} %reshape.116), channel_id=1, replica_groups=mesh['species'=16,'tile'=16] {'species'}, dimensions={1} | all-to-all | bytes 1048576 | tf_op jit(solution)/shard_map/all_to_all | solution.py:77
  117.9 3.6 %all-to-all-start.1 = ((bf16[16,2,8192]{2,1,0:T(2,128)(2,1)}), bf16[16,2,8192]{2,1,0:T(2,128)(2,1)S(1)}, u32[]{:S(2)}, u32[]{:S(2)}) async-start(bf16[16,2,8192]{2,1,0:T(2,128)(2,1)} %reshape.176), calls=%async_computation.1 | async-start | bytes 1048576 | tf_op jit(solution)/shard_map/all_to_all | solution.py:84
  122.9 9.4 %all-to-all-done.1 = bf16[16,2,8192]{2,1,0:T(2,128)(2,1)S(1)} async-done(((bf16[16,2,8192]{2,1,0:T(2,128)(2,1)}), bf16[16,2,8192]{2,1,0:T(2,128)(2,1)S(1)}, u32[]{:S(2)}, u32[]{:S(2)}) %all-to-all-start.1) | async-done | bytes 524320 | tf_op jit(solution)/shard_map/all_to_all | solution.py:84
  136.0 4.8 %collective-permute-start.2 = (f32[17,16,1,128]{3,1,2,0:T(8,128)S(1)}, f32[17,16,1,128]{3,1,2,0:T(8,128)S(1)}, u32[]{:S(2)}, u32[]{:S(2)}) collective-permute-start(f32[17,16,1,128]{3,1,2,0:T(8,128)S(1)} %get-tuple-element.17), channel_id=1, source_target_pairs={{0,1},{1,2},{2,3},{3,4},{4,5},{5,6},{6,7},{7,8},{8,9},{9,10},{10,1... | collective-permute-start | bytes 417800 | tf_op jit(solution)/shard_map/ppermute | solution.py:17
  141.6 3.2 %collective-permute-done.3 = f32[17,16,1,128]{3,1,2,0:T(8,128)S(1)} collective-permute-done((f32[17,16,1,128]{3,1,2,0:T(8,128)S(1)}, f32[17,16,1,128]{3,1,2,0:T(8,128)S(1)}, u32[]{:S(2)}, u32[]{:S(2)}) %collective-permute-start.3) | collective-permute-done | bytes 139296 | tf_op jit(solution)/shard_map/ppermute | solution.py:19
  144.7 3.8 %collective-permute-done.2 = f32[17,16,1,128]{3,1,2,0:T(8,128)S(1)} collective-permute-done((f32[17,16,1,128]{3,1,2,0:T(8,128)S(1)}, f32[17,16,1,128]{3,1,2,0:T(8,128)S(1)}, u32[]{:S(2)}, u32[]{:S(2)}) %collective-permute-start.2) | collective-permute-done | bytes 139296 | tf_op jit(solution)/shard_map/ppermute | solution.py:17
  151.0 14.3 %all_to_all.97 = bf16[16,16,1024]{2,0,1:T(8,128)(2,1)S(1)} all-to-all(bf16[16,16,1024]{2,0,1:T(8,128)(2,1)S(1)} %reshape.118), channel_id=1, replica_groups=mesh['species'=16,'tile'=16] {'species'}, dimensions={1} | all-to-all | bytes 1048576 | tf_op jit(solution)/shard_map/all_to_all | solution.py:77
  168.6 3.6 %all-to-all-start.3 = ((bf16[16,2,8192]{2,1,0:T(2,128)(2,1)}), bf16[16,2,8192]{2,1,0:T(2,128)(2,1)S(1)}, u32[]{:S(2)}, u32[]{:S(2)}) async-start(bf16[16,2,8192]{2,1,0:T(2,128)(2,1)} %reshape.178), calls=%async_computation.3 | async-start | bytes 1048576 | tf_op jit(solution)/shard_map/all_to_all | solution.py:84
  173.0 10.0 %all-to-all-done.3 = bf16[16,2,8192]{2,1,0:T(2,128)(2,1)S(1)} async-done(((bf16[16,2,8192]{2,1,0:T(2,128)(2,1)}), bf16[16,2,8192]{2,1,0:T(2,128)(2,1)S(1)}, u32[]{:S(2)}, u32[]{:S(2)}) %all-to-all-start.3) | async-done | bytes 524320 | tf_op jit(solution)/shard_map/all_to_all | solution.py:84
  186.7 4.8 %collective-permute-start.4 = (f32[17,16,1,128]{3,1,2,0:T(8,128)S(1)}, f32[17,16,1,128]{3,1,2,0:T(8,128)S(1)}, u32[]{:S(2)}, u32[]{:S(2)}) collective-permute-start(f32[17,16,1,128]{3,1,2,0:T(8,128)S(1)} %get-tuple-element.15), channel_id=1, source_target_pairs={{0,1},{1,2},{2,3},{3,4},{4,5},{5,6},{6,7},{7,8},{8,9},{9,10},{10,1... | collective-permute-start | bytes 417800 | tf_op jit(solution)/shard_map/ppermute | solution.py:17
  193.7 4.3 %collective-permute-done.4 = f32[17,16,1,128]{3,1,2,0:T(8,128)S(1)} collective-permute-done((f32[17,16,1,128]{3,1,2,0:T(8,128)S(1)}, f32[17,16,1,128]{3,1,2,0:T(8,128)S(1)}, u32[]{:S(2)}, u32[]{:S(2)}) %collective-permute-start.4) | collective-permute-done | bytes 139296 | tf_op jit(solution)/shard_map/ppermute | solution.py:17
  199.8 15.5 %all_to_all.98 = bf16[16,16,1024]{2,0,1:T(8,128)(2,1)S(1)} all-to-all(bf16[16,16,1024]{2,0,1:T(8,128)(2,1)S(1)} %reshape.120), channel_id=1, replica_groups=mesh['species'=16,'tile'=16] {'species'}, dimensions={1} | all-to-all | bytes 1048576 | tf_op jit(solution)/shard_map/all_to_all | solution.py:77
  218.7 3.6 %all-to-all-start.5 = ((bf16[16,2,8192]{2,1,0:T(2,128)(2,1)}), bf16[16,2,8192]{2,1,0:T(2,128)(2,1)S(1)}, u32[]{:S(2)}, u32[]{:S(2)}) async-start(bf16[16,2,8192]{2,1,0:T(2,128)(2,1)} %reshape.180), calls=%async_computation.5 | async-start | bytes 1048576 | tf_op jit(solution)/shard_map/all_to_all | solution.py:84
  222.5 10.6 %all-to-all-done.5 = bf16[16,2,8192]{2,1,0:T(2,128)(2,1)S(1)} async-done(((bf16[16,2,8192]{2,1,0:T(2,128)(2,1)}), bf16[16,2,8192]{2,1,0:T(2,128)(2,1)S(1)}, u32[]{:S(2)}, u32[]{:S(2)}) %all-to-all-start.5) | async-done | bytes 524320 | tf_op jit(solution)/shard_map/all_to_all | solution.py:84
  236.9 5.0 %collective-permute-start.6 = (f32[17,16,1,128]{3,1,2,0:T(8,128)S(1)}, f32[17,16,1,128]{3,1,2,0:T(8,128)S(1)}, u32[]{:S(2)}, u32[]{:S(2)}) collective-permute-start(f32[17,16,1,128]{3,1,2,0:T(8,128)S(1)} %get-tuple-element.13), channel_id=1, source_target_pairs={{0,1},{1,2},{2,3},{3,4},{4,5},{5,6},{6,7},{7,8},{8,9},{9,10},{10,1... | collective-permute-start | bytes 417800 | tf_op jit(solution)/shard_map/ppermute | solution.py:17
  242.9 4.4 %collective-permute-done.6 = f32[17,16,1,128]{3,1,2,0:T(8,128)S(1)} collective-permute-done((f32[17,16,1,128]{3,1,2,0:T(8,128)S(1)}, f32[17,16,1,128]{3,1,2,0:T(8,128)S(1)}, u32[]{:S(2)}, u32[]{:S(2)}) %collective-permute-start.6) | collective-permute-done | bytes 139296 | tf_op jit(solution)/shard_map/ppermute | solution.py:17
  249.1 16.4 %all_to_all.99 = bf16[16,16,1024]{2,0,1:T(8,128)(2,1)S(1)} all-to-all(bf16[16,16,1024]{2,0,1:T(8,128)(2,1)S(1)} %reshape.122), channel_id=1, replica_groups=mesh['species'=16,'tile'=16] {'species'}, dimensions={1} | all-to-all | bytes 1048576 | tf_op jit(solution)/shard_map/all_to_all | solution.py:77
  268.1 13.5 %all_to_all.100 = bf16[16,2,8192]{2,1,0:T(2,128)(2,1)S(1)} all-to-all(bf16[16,2,8192]{2,1,0:T(2,128)(2,1)S(1)} %reshape.182), channel_id=1, replica_groups=mesh['species'=16,'tile'=16] {'species'}, dimensions={0} | all-to-all | bytes 1048576 | tf_op jit(solution)/shard_map/all_to_all | solution.py:84
  (156 shorter events, 50.2 us)
Async XLA Ops:
  0.0 114.0 %copy-start = (bf16[256,512]{1,0:T(8,128)(2,1)S(1)}, bf16[256,512]{1,0:T(8,128)(2,1)}, u32[]{:S(2)}) copy-start(bf16[256,512]{1,0:T(8,128)(2,1)} %param.7) | copy-start | bytes 786436
  0.0 75.9 %copy-start.1 = (f32[16,16,8,128]{3,2,1,0:T(8,128)S(1)}, f32[16,16,8,128]{3,2,1,0:T(8,128)}, u32[]{:S(2)}) copy-start(f32[16,16,8,128]{3,2,1,0:T(8,128)} %param.4) | copy-start | bytes 3145732
  77.8 12.5 %collective-permute-start.1 = (f32[17,16,1,128]{3,1,2,0:T(8,128)S(1)}, f32[17,16,1,128]{3,1,2,0:T(8,128)S(1)}, u32[]{:S(2)}, u32[]{:S(2)}) collective-permute-start(f32[17,16,1,128]{3,1,2,0:T(8,128)S(1)} %get-tuple-element.20), channel_id=1, source_target_pairs={{1,0},{2,1},{3,2},{4,3},{5,4},{6,5},{7,6},{8,7},{9,8},{10,9},{11,1... | collective-permute-start | bytes 417800 | tf_op jit(solution)/shard_map/ppermute | solution.py:19
  85.1 13.5 %collective-permute-start = (f32[17,16,1,128]{3,1,2,0:T(8,128)S(1)}, f32[17,16,1,128]{3,1,2,0:T(8,128)S(1)}, u32[]{:S(2)}, u32[]{:S(2)}) collective-permute-start(f32[17,16,1,128]{3,1,2,0:T(8,128)S(1)} %get-tuple-element.19), channel_id=1, source_target_pairs={{0,1},{1,2},{2,3},{3,4},{4,5},{5,6},{6,7},{7,8},{8,9},{9,10},{10,1... | collective-permute-start | bytes 417800 | tf_op jit(solution)/shard_map/ppermute | solution.py:17
  100.1 13.8 %copy-start.13 = (bf16[512,256]{1,0:T(8,128)(2,1)S(1)}, bf16[512,256]{1,0:T(8,128)(2,1)}, u32[]{:S(2)}) copy-start(bf16[512,256]{1,0:T(8,128)(2,1)} %param.6) | copy-start | bytes 786436
  116.7 5.5 %copy-start.6 = (f32[17,8,128]{2,1,0:T(8,128)S(1)}, f32[17,8,128]{2,1,0:T(8,128)}, u32[]{:S(2)}) copy-start(f32[17,8,128]{2,1,0:T(8,128)} %get-tuple-element.60) | copy-start | bytes 208900
  117.9 14.4 %all-to-all-start.1 = ((bf16[16,2,8192]{2,1,0:T(2,128)(2,1)}), bf16[16,2,8192]{2,1,0:T(2,128)(2,1)S(1)}, u32[]{:S(2)}, u32[]{:S(2)}) async-start(bf16[16,2,8192]{2,1,0:T(2,128)(2,1)} %reshape.176), calls=%async_computation.1 | async-start | bytes 1048576 | tf_op jit(solution)/shard_map/all_to_all | solution.py:84
  134.1 10.6 %collective-permute-start.3 = (f32[17,16,1,128]{3,1,2,0:T(8,128)S(1)}, f32[17,16,1,128]{3,1,2,0:T(8,128)S(1)}, u32[]{:S(2)}, u32[]{:S(2)}) collective-permute-start(f32[17,16,1,128]{3,1,2,0:T(8,128)S(1)} %get-tuple-element.18), channel_id=1, source_target_pairs={{1,0},{2,1},{3,2},{4,3},{5,4},{6,5},{7,6},{8,7},{9,8},{10,9},{11,1... | collective-permute-start | bytes 417800 | tf_op jit(solution)/shard_map/ppermute | solution.py:19
  136.0 12.5 %collective-permute-start.2 = (f32[17,16,1,128]{3,1,2,0:T(8,128)S(1)}, f32[17,16,1,128]{3,1,2,0:T(8,128)S(1)}, u32[]{:S(2)}, u32[]{:S(2)}) collective-permute-start(f32[17,16,1,128]{3,1,2,0:T(8,128)S(1)} %get-tuple-element.17), channel_id=1, source_target_pairs={{0,1},{1,2},{2,3},{3,4},{4,5},{5,6},{6,7},{7,8},{8,9},{9,10},{10,1... | collective-permute-start | bytes 417800 | tf_op jit(solution)/shard_map/ppermute | solution.py:17
  150.6 14.7 %copy-start.14 = (bf16[512,256]{1,0:T(8,128)(2,1)S(1)}, bf16[512,256]{1,0:T(8,128)(2,1)}, u32[]{:S(2)}) copy-start(bf16[512,256]{1,0:T(8,128)(2,1)} %param.6) | copy-start | bytes 786436
  167.2 5.0 %copy-start.11 = (f32[1,16,8,128]{3,2,1,0:T(8,128)S(1)}, f32[1,16,8,128]{3,2,1,0:T(8,128)}, u32[]{:S(2)}) copy-start(f32[1,16,8,128]{3,2,1,0:T(8,128)} %get-tuple-element.57) | copy-start | bytes 196612
  167.2 5.0 %copy-start.8 = (f32[16,8,128]{2,1,0:T(8,128)S(1)}, f32[16,8,128]{2,1,0:T(8,128)}, u32[]{:S(2)}) copy-start(f32[16,8,128]{2,1,0:T(8,128)} %get-tuple-element.51) | copy-start | bytes 196612
  167.2 5.0 %copy-start.9 = (f32[16,8,128]{2,1,0:T(8,128)S(1)}, f32[16,8,128]{2,1,0:T(8,128)}, u32[]{:S(2)}) copy-start(f32[16,8,128]{2,1,0:T(8,128)} %get-tuple-element.53) | copy-start | bytes 196612
  168.6 14.4 %all-to-all-start.3 = ((bf16[16,2,8192]{2,1,0:T(2,128)(2,1)}), bf16[16,2,8192]{2,1,0:T(2,128)(2,1)S(1)}, u32[]{:S(2)}, u32[]{:S(2)}) async-start(bf16[16,2,8192]{2,1,0:T(2,128)(2,1)} %reshape.178), calls=%async_computation.3 | async-start | bytes 1048576 | tf_op jit(solution)/shard_map/all_to_all | solution.py:84
  184.8 9.0 %collective-permute-start.5 = (f32[17,16,1,128]{3,1,2,0:T(8,128)S(1)}, f32[17,16,1,128]{3,1,2,0:T(8,128)S(1)}, u32[]{:S(2)}, u32[]{:S(2)}) collective-permute-start(f32[17,16,1,128]{3,1,2,0:T(8,128)S(1)} %get-tuple-element.16), channel_id=1, source_target_pairs={{1,0},{2,1},{3,2},{4,3},{5,4},{6,5},{7,6},{8,7},{9,8},{10,9},{11,1... | collective-permute-start | bytes 417800 | tf_op jit(solution)/shard_map/ppermute | solution.py:19
  186.7 11.3 %collective-permute-start.4 = (f32[17,16,1,128]{3,1,2,0:T(8,128)S(1)}, f32[17,16,1,128]{3,1,2,0:T(8,128)S(1)}, u32[]{:S(2)}, u32[]{:S(2)}) collective-permute-start(f32[17,16,1,128]{3,1,2,0:T(8,128)S(1)} %get-tuple-element.15), channel_id=1, source_target_pairs={{0,1},{1,2},{2,3},{3,4},{4,5},{5,6},{6,7},{7,8},{8,9},{9,10},{10,1... | collective-permute-start | bytes 417800 | tf_op jit(solution)/shard_map/ppermute | solution.py:17
  199.4 15.9 %copy-start.15 = (bf16[512,256]{1,0:T(8,128)(2,1)S(1)}, bf16[512,256]{1,0:T(8,128)(2,1)}, u32[]{:S(2)}) copy-start(bf16[512,256]{1,0:T(8,128)(2,1)} %param.6) | copy-start | bytes 786436
  217.3 5.0 %copy-start.10 = (f32[1,16,8,128]{3,2,1,0:T(8,128)S(1)}, f32[1,16,8,128]{3,2,1,0:T(8,128)}, u32[]{:S(2)}) copy-start(f32[1,16,8,128]{3,2,1,0:T(8,128)} %get-tuple-element.58) | copy-start | bytes 196612
  217.3 5.0 %copy-start.5 = (f32[17,8,128]{2,1,0:T(8,128)S(1)}, f32[17,8,128]{2,1,0:T(8,128)}, u32[]{:S(2)}) copy-start(f32[17,8,128]{2,1,0:T(8,128)} %get-tuple-element.61) | copy-start | bytes 208900
  217.3 5.0 %copy-start.4 = (f32[17,8,128]{2,1,0:T(8,128)S(1)}, f32[17,8,128]{2,1,0:T(8,128)}, u32[]{:S(2)}) copy-start(f32[17,8,128]{2,1,0:T(8,128)} %get-tuple-element.62) | copy-start | bytes 208900
  218.7 14.4 %all-to-all-start.5 = ((bf16[16,2,8192]{2,1,0:T(2,128)(2,1)}), bf16[16,2,8192]{2,1,0:T(2,128)(2,1)S(1)}, u32[]{:S(2)}, u32[]{:S(2)}) async-start(bf16[16,2,8192]{2,1,0:T(2,128)(2,1)} %reshape.180), calls=%async_computation.5 | async-start | bytes 1048576 | tf_op jit(solution)/shard_map/all_to_all | solution.py:84
  234.9 8.0 %collective-permute-start.7 = (f32[17,16,1,128]{3,1,2,0:T(8,128)S(1)}, f32[17,16,1,128]{3,1,2,0:T(8,128)S(1)}, u32[]{:S(2)}, u32[]{:S(2)}) collective-permute-start(f32[17,16,1,128]{3,1,2,0:T(8,128)S(1)} %get-tuple-element.14), channel_id=1, source_target_pairs={{1,0},{2,1},{3,2},{4,3},{5,4},{6,5},{7,6},{8,7},{9,8},{10,9},{11,1... | collective-permute-start | bytes 417800 | tf_op jit(solution)/shard_map/ppermute | solution.py:19
  236.9 10.4 %collective-permute-start.6 = (f32[17,16,1,128]{3,1,2,0:T(8,128)S(1)}, f32[17,16,1,128]{3,1,2,0:T(8,128)S(1)}, u32[]{:S(2)}, u32[]{:S(2)}) collective-permute-start(f32[17,16,1,128]{3,1,2,0:T(8,128)S(1)} %get-tuple-element.13), channel_id=1, source_target_pairs={{0,1},{1,2},{2,3},{3,4},{4,5},{5,6},{6,7},{7,8},{8,9},{9,10},{10,1... | collective-permute-start | bytes 417800 | tf_op jit(solution)/shard_map/ppermute | solution.py:17
  248.7 16.8 %copy-start.16 = (bf16[512,256]{1,0:T(8,128)(2,1)S(1)}, bf16[512,256]{1,0:T(8,128)(2,1)}, u32[]{:S(2)}) copy-start(bf16[512,256]{1,0:T(8,128)(2,1)} %param.6) | copy-start | bytes 786436
  (4 other events, 11.4 us)
where the time goes:
time: 285 us; the launch traced here: 284 us
  blocking collectives  147 us (52%)
  waiting for transfers between devices  57.1 us (20%)
  starting transfers between devices  40.4 us (14%)
  local copies, waits for them, and re-layouts  18.7 us (7%)
  other arithmetic  17.2 us (6%)
  matrix products  3.48 us (1%)
    all_gather x4, blocking collectives, per_device(): gathered = lax.all_gather(fluxes[interval], 'species', axis=1, tiled=True)  73.5 us
    all_to_all x4, blocking collectives, per_device(): lax.all_to_all(flattened, 'species', split_axis=1, concat_axis=0, tiled=T...  59.7 us
    all_to_all x3, waiting for transfers between devices, per_device(): lax.all_to_all(tendency, 'species', split_axis=0, concat_axis=1, tiled=True)  30 us
    ppermute x4, waiting for transfers between devices, extended(): lax.ppermute(tail, axis, [(i, (i + 1) % count) for i in range(ends)])  20.7 us
    ppermute x4, starting transfers between devices, extended(): lax.ppermute(tail, axis, [(i, (i + 1) % count) for i in range(ends)])  16.6 us
    all_to_all x1, blocking collectives, per_device(): lax.all_to_all(tendency, 'species', split_axis=0, concat_axis=1, tiled=True)  13.5 us
    ppermute x4, starting transfers between devices, extended(): lax.ppermute(head, axis, [((i + 1) % count, i) for i in range(ends)])  13 us
    all_to_all x3, starting transfers between devices, per_device(): lax.all_to_all(tendency, 'species', split_axis=0, concat_axis=1, tiled=True)  10.7 us
  transfers between devices with their start and end apart: 11, of which 11 were waited for; matrix products, arithmetic and copies ran while one was open for 2% of the time, Pallas kernels for 0%

commit v1 on v0

v1 whole, which is shorter than its diff:
```python
import functools

import jax
import jax.numpy as jnp
from jax import lax
from jax.experimental import pallas as pl
from jax.experimental.pallas import tpu as pltpu
from jax.sharding import PartitionSpec as P

STEPS = 4
GROUP = 16
TILES = 16
LANES = 128
SPEC = 256
OWN = 16
BLOCK = 8
CHUNKS = 4
F32 = jnp.float32
BF16 = jnp.bfloat16
MESH = pl.DeviceIdType.MESH


def device_of(block):
    place = block // 2
    half = place // 4
    row = jnp.where(half == 0, place, 7 - place)
    return 4 * row + 2 * half + block % 2


def block_of(device):
    row = device // 4
    half = (device // 2) % 2
    place = jnp.where(half == 0, row, 7 - row)
    return 2 * place + device % 2


def transport(
    tracers, fluxes, weight_in, weight_out, back,
    turned, sent, flux_out, flux_own, flux_next, edge_out, edge_in, arrived,
    state, coeff, xs_out, xs_in, ys_out, ys_in, cells, hidden, result,
    flux_send, flux_recv, main_send, main_recv, edge_send, edge_recv,
    x_send, x_recv, y_send, y_recv, back_send, back_recv,
):
    spec = lax.axis_index("species")
    tile = lax.axis_index("tile")
    block = block_of(spec)
    right_tile = lax.rem(tile + 1, TILES)
    left_tile = lax.rem(tile + TILES - 1, TILES)
    upper = device_of(lax.rem(block + 1, GROUP))
    lower = device_of(lax.rem(block + GROUP - 1, GROUP))

    barrier = pltpu.get_barrier_semaphore()

    def greet(k, carry):
        peer = lax.rem(spec + k, GROUP)

        @pl.when(k > 0)
        def _():
            pl.semaphore_signal(barrier, inc=1, device_id=(peer, tile), device_id_type=MESH)

        pl.semaphore_signal(barrier, inc=1, device_id=(peer, left_tile), device_id_type=MESH)
        pl.semaphore_signal(barrier, inc=1, device_id=(peer, right_tile), device_id_type=MESH)
        return carry

    lax.fori_loop(0, GROUP, greet, 0)

    rows = []
    for step in range(STEPS):
        along_y = fluxes[step, 1, 0]
        rows += [fluxes[step, 0, 0], along_y, fluxes[step, 2, 0], pltpu.roll(along_y, LANES - 1, 1)]
    flux_out[...] = jnp.concatenate(rows, 0).T

    def turn(own, carry):
        turned[pl.ds(own, LANES, stride=OWN), :] = tracers[own].reshape(LANES, LANES).T
        return carry

    lax.fori_loop(0, OWN, turn, 0)

    def narrow(y, carry):
        sent[y + 1] = turned[pl.ds(y * OWN, OWN), :].astype(BF16)
        return carry

    lax.fori_loop(0, LANES, narrow, 0, unroll=8)
    sent[0] = turned[pl.ds((LANES - 1) * OWN, OWN), :].astype(BF16)
    sent[LANES + 1] = turned[pl.ds(0, OWN), :].astype(BF16)

    pl.semaphore_wait(barrier, 3 * GROUP - 1)

    def flux_copy(k, home):
        peer = lax.rem(spec + k, GROUP)
        return pltpu.make_async_remote_copy(
            src_ref=flux_out.at[pl.ds(pl.multiple_of(block_of(peer) * BLOCK, BLOCK), BLOCK)],
            dst_ref=(flux_own if home else flux_next).at[spec],
            send_sem=flux_send.at[0 if home else 1, k],
            recv_sem=flux_recv.at[0 if home else 1],
            device_id=(peer, tile if home else left_tile),
            device_id_type=MESH,
        )

    def main_copy(k):
        peer = lax.rem(spec + k, GROUP)
        return pltpu.make_async_remote_copy(
            src_ref=sent.at[pl.ds(block_of(peer) * BLOCK, BLOCK + 2)],
            dst_ref=arrived.at[:, pl.ds(pl.multiple_of(spec * OWN, OWN), OWN)],
            send_sem=main_send.at[k],
            recv_sem=main_recv,
            device_id=(peer, tile),
            device_id_type=MESH,
        )

    own_flux = pltpu.make_async_copy(
        flux_out.at[pl.ds(pl.multiple_of(block * BLOCK, BLOCK), BLOCK)], flux_own.at[spec], flux_recv.at[0]
    )
    own_main = pltpu.make_async_copy(
        sent.at[pl.ds(block * BLOCK, BLOCK + 2)],
        arrived.at[:, pl.ds(pl.multiple_of(spec * OWN, OWN), OWN)],
        main_recv,
    )

    own_flux.start()

    def send_flux(k, carry):
        @pl.when(k > 0)
        def _():
            flux_copy(k, True).start()

        flux_copy(k, False).start()
        return carry

    lax.fori_loop(0, GROUP, send_flux, 0)
    own_main.start()

    def send_main(k, carry):
        main_copy(k).start()
        return carry

    lax.fori_loop(1, GROUP, send_main, 0)

    lane = lax.broadcasted_iota(jnp.int32, (1, LANES), 1)
    at_x = lane % 8
    at_z = lane // 8

    def edge_copy(k, side):
        peer = lax.rem(spec + k, GROUP)
        return pltpu.make_async_remote_copy(
            src_ref=edge_out.at[side, block_of(peer)],
            dst_ref=edge_in.at[side, pl.ds(pl.multiple_of(spec * OWN, OWN), OWN)],
            send_sem=edge_send.at[side, k],
            recv_sem=edge_recv.at[side],
            device_id=(peer, right_tile if side == 0 else left_tile),
            device_id_type=MESH,
        )

    def pack_edges(to, carry):
        base = to * (BLOCK * OWN)
        high = jnp.zeros((OWN, LANES), F32)
        low = jnp.zeros((OWN, LANES), F32)
        for y in range(BLOCK):
            value = turned[pl.ds(base + y * OWN, OWN), :]
            high = jnp.where(at_x == y, pltpu.roll(value, (y - 7) % LANES, 1), high)
            low = jnp.where(at_x == y, pltpu.roll(value, y, 1) if y else value, low)
        edge_out[0, to] = high.astype(BF16)
        edge_out[1, to] = low.astype(BF16)
        return carry

    lax.fori_loop(0, GROUP, pack_edges, 0)

    def send_edges(k, carry):
        edge_copy(k, 0).start()
        edge_copy(k, 1).start()
        return carry

    lax.fori_loop(0, GROUP, send_edges, 0)

    pltpu.make_async_copy(flux_own, flux_own, flux_recv.at[0]).wait()
    pltpu.make_async_copy(flux_next, flux_next, flux_recv.at[1]).wait()
    for step in range(STEPS):
        fields = []
        for field in range(4):
            value = jnp.zeros((BLOCK, LANES), F32)
            for level in range(16):
                shift = (level * 8 - (step * 4 + field) * 8) % LANES
                piece = flux_own[level]
                value = jnp.where(at_z == level, pltpu.roll(piece, shift, 1) if shift else piece, value)
            fields.append(value)
        flux_x, flux_y, flux_z, flux_y_up = fields
        beyond = jnp.zeros((BLOCK, LANES), F32)
        for level in range(16):
            shift = (level * 8 + 7 - step * 32) % LANES
            beyond = jnp.where(at_z == level, pltpu.roll(flux_next[level], shift, 1), beyond)
        flux_x = jnp.where((at_x == 0) & (tile == 0), 0.0, flux_x)
        beyond = jnp.where(tile == TILES - 1, 0.0, beyond)
        flux_z = jnp.where(at_z == 0, 0.0, flux_z)
        flux_x_up = jnp.where(at_x == 7, beyond, pltpu.roll(flux_x, LANES - 1, 1))
        flux_z_up = pltpu.roll(flux_z, LANES - 8, 1)
        lows = [jnp.minimum(f, 0.0) for f in (flux_x, flux_y, flux_z)]
        highs = [jnp.maximum(f, 0.0) for f in (flux_x_up, flux_y_up, flux_z_up)]
        centre = 1.0 + (lows[0] - highs[0]) + (lows[1] - highs[1]) + (lows[2] - highs[2])
        terms = [
            centre,
            jnp.maximum(flux_x, 0.0), -jnp.minimum(flux_x_up, 0.0),
            jnp.maximum(flux_y, 0.0), -jnp.minimum(flux_y_up, 0.0),
            jnp.maximum(flux_z, 0.0), -jnp.minimum(flux_z_up, 0.0),
        ]
        for which, term in enumerate(terms):
            coeff[pl.ds(step * 64 + which, BLOCK, stride=8), :] = term

    pltpu.make_async_copy(arrived, arrived, main_recv).wait()

    def widen(row, carry):
        at = pl.ds(pl.multiple_of(row * 32, 32), 32)
        for slab in range(BLOCK + 2):
            state[0, slab, at] = arrived[slab, at].astype(F32)
        return carry

    lax.fori_loop(0, SPEC // 32, widen, 0)
    for side in range(2):
        pltpu.make_async_copy(edge_in.at[side], edge_in.at[side], edge_recv.at[side]).wait()

    def repack(row, carry):
        at = pl.multiple_of(row * 16, 16)
        for side in range(2):
            values = [edge_in[side, pl.ds(q * 64 + at, 16)].astype(F32) for q in range(4)]
            for chunk in range(CHUNKS):
                value = jnp.zeros((16, LANES), F32)
                for q in range(4):
                    shift = (2 * q - 2 * chunk) % LANES
                    moved = pltpu.roll(values[q], shift, 1) if shift else values[q]
                    value = jnp.where(at_x // 2 == q, moved, value)
                xs_in[0, chunk, side, pl.ds(at, 16)] = value.astype(BF16)
        return carry

    lax.fori_loop(0, 4, repack, 0)

    def x_copy(step, chunk, side):
        return pltpu.make_async_remote_copy(
            src_ref=xs_out.at[step, chunk, side],
            dst_ref=xs_in.at[step + 1, chunk, side],
            send_sem=x_send.at[step, chunk, side],
            recv_sem=x_recv.at[step, chunk, side],
            device_id=(spec, right_tile if side == 0 else left_tile),
            device_id_type=MESH,
        )

    def y_copy(step, side):
        return pltpu.make_async_remote_copy(
            src_ref=ys_out.at[step, side],
            dst_ref=ys_in.at[step, side],
            send_sem=y_send.at[step, side],
            recv_sem=y_recv.at[step, side],
            device_id=(upper if side == 0 else lower, tile),
            device_id_type=MESH,
        )

    def back_copy(chunk, k):
        peer = lax.rem(spec + k, GROUP)
        return pltpu.make_async_remote_copy(
            src_ref=result.at[pl.ds(2 * chunk, 2), pl.ds(pl.multiple_of(peer * OWN, OWN), OWN)],
            dst_ref=back.at[pl.ds(block * BLOCK + 2 * chunk, 2)],
            send_sem=back_send.at[chunk, k],
            recv_sem=back_recv,
            device_id=(peer, tile),
            device_id_type=MESH,
        )

    def own_back(chunk):
        return pltpu.make_async_copy(
            result.at[pl.ds(2 * chunk, 2), pl.ds(pl.multiple_of(spec * OWN, OWN), OWN)],
            back.at[pl.ds(block * BLOCK + 2 * chunk, 2)],
            back_recv,
        )

    def halo_slab(step, now, side):
        y_copy(step - 1, side).wait_recv()

        def one(row, carry):
            at = pl.ds(pl.multiple_of(row * 32, 32), 32)
            state[now, 0 if side == 0 else BLOCK + 1, at] = ys_in[step - 1, side, at].astype(F32)
            return carry

        lax.fori_loop(0, SPEC // 32, one, 0)

    def do_chunk(step, order):
        chunk = jnp.where(order == 0, 0, jnp.where(order == 1, CHUNKS - 1, order - 1))
        now = lax.rem(step, 2)
        later = 1 - now

        @pl.when(step > 0)
        def _():
            x_copy(step - 1, chunk, 0).wait_recv()
            x_copy(step - 1, chunk, 1).wait_recv()

            @pl.when(chunk == 0)
            def _():
                halo_slab(step, now, 0)

            @pl.when(chunk == CHUNKS - 1)
            def _():
                halo_slab(step, now, 1)

        for yy in range(2):
            y = 2 * chunk + yy
            table = coeff[pl.ds(pl.multiple_of((step * BLOCK + y) * 8, 8), 8), :]
            ks = [table[i:i + 1] for i in range(7)]

            def rows_of(part, carry, yy=yy, y=y, ks=ks):
                off = pl.multiple_of(part * 32, 32)
                halo_l = xs_in[step, chunk, 0, pl.ds(off, 32)].astype(F32)
                halo_r = xs_in[step, chunk, 1, pl.ds(off, 32)].astype(F32)
                for q in range(4):
                    slot = 2 * q + yy
                    at = pl.ds(off + q * 64, 32)
                    here = state[now, y + 1, at]
                    from_l = pltpu.roll(halo_l, LANES - slot, 1) if slot else halo_l
                    from_r = pltpu.roll(halo_r, 7 - slot, 1) if slot < 7 else halo_r
                    left = jnp.where(at_x == 0, from_l, pltpu.roll(here, 1, 1))
                    right = jnp.where(at_x == 7, from_r, pltpu.roll(here, LANES - 1, 1))
                    new = ks[0] * here + ks[1] * left + ks[2] * right
                    new += ks[3] * state[now, y, at] + ks[4] * state[now, y + 2, at]
                    new += ks[5] * pltpu.roll(here, 8, 1) + ks[6] * pltpu.roll(here, LANES - 8, 1)
                    state[later, y + 1, at] = new
                    cells[at, yy * LANES:(yy + 1) * LANES] = new.astype(BF16)
                return carry

            lax.fori_loop(0, 2, rows_of, 0)

        pre = jnp.dot(weight_in[...], cells[...], preferred_element_type=F32)
        hidden[...] = (0.5 * pre * (1.0 + jnp.tanh(0.5 * pre))).astype(BF16)
        change = (0.5 * jnp.dot(weight_out[...], hidden[...], preferred_element_type=F32)).astype(BF16).astype(F32)
        for yy in range(2):
            state[later, 2 * chunk + yy + 1] += change[:, yy * LANES:(yy + 1) * LANES]

        @pl.when(step < STEPS - 1)
        def _():
            def pack(part, carry):
                off = pl.multiple_of(part * 16, 16)
                high = jnp.zeros((16, LANES), F32)
                low = jnp.zeros((16, LANES), F32)
                for q in range(4):
                    for yy in range(2):
                        slot = 2 * q + yy
                        value = state[later, 2 * chunk + yy + 1, pl.ds(off + q * 64, 16)]
                        high = jnp.where(at_x == slot, pltpu.roll(value, (slot - 7) % LANES, 1), high)
                        low = jnp.where(at_x == slot, pltpu.roll(value, slot, 1) if slot else value, low)
                xs_out[step, chunk, 0, pl.ds(off, 16)] = high.astype(BF16)
                xs_out[step, chunk, 1, pl.ds(off, 16)] = low.astype(BF16)
                return carry

            lax.fori_loop(0, 4, pack, 0)
            x_copy(step, chunk, 0).start()
            x_copy(step, chunk, 1).start()

            @pl.when(chunk == 0)
            def _():
                ys_out[step, 1] = state[later, 1].astype(BF16)
                y_copy(step, 1).start()

            @pl.when(chunk == CHUNKS - 1)
            def _():
                ys_out[step, 0] = state[later, BLOCK].astype(BF16)
                y_copy(step, 0).start()

        @pl.when(step == STEPS - 1)
        def _():
            for yy in range(2):
                result[2 * chunk + yy] = state[later, 2 * chunk + yy + 1].astype(BF16)
            own_back(chunk).start()

            def send_back(k, carry):
                back_copy(chunk, k).start()
                return carry

            lax.fori_loop(1, GROUP, send_back, 0)

    def do_step(step, carry):
        def one(order, inner):
            do_chunk(step, order)
            return inner

        lax.fori_loop(0, CHUNKS, one, 0)
        return carry

    lax.fori_loop(0, STEPS, do_step, 0)

    def sent_out(k, carry):
        flux_copy(k, False).wait_send()
        edge_copy(k, 0).wait_send()
        edge_copy(k, 1).wait_send()

        @pl.when(k > 0)
        def _():
            flux_copy(k, True).wait_send()
            main_copy(k).wait_send()

        return carry

    lax.fori_loop(0, GROUP, sent_out, 0)
    for step in range(STEPS - 1):
        for side in range(2):
            y_copy(step, side).wait_send()
            for chunk in range(CHUNKS):
                x_copy(step, chunk, side).wait_send()

    def back_out(k, carry):
        for chunk in range(CHUNKS):
            back_copy(chunk, k).wait_send()
        return carry

    lax.fori_loop(1, GROUP, back_out, 0)
    pltpu.make_async_copy(back, back, back_recv).wait()


def turn_back(back, out, wide):
    def widen(y, carry):
        wide[pl.ds(pl.multiple_of(y * OWN, OWN), OWN), :] = back[y].astype(F32)
        return carry

    lax.fori_loop(0, LANES, widen, 0, unroll=8)

    def one(own, carry):
        out[own] = wide[pl.ds(own, LANES, stride=OWN), :].T.reshape(16, 8, LANES)
        return carry

    lax.fori_loop(0, OWN, one, 0)


def per_device(tracers, fluxes, weight_in, weight_out):
    vmem = pl.BlockSpec(memory_space=pltpu.VMEM)
    dma = pltpu.SemaphoreType.DMA
    back = pl.pallas_call(
        transport,
        out_shape=jax.ShapeDtypeStruct((LANES, OWN, LANES), BF16),
        in_specs=[vmem] * 4,
        out_specs=pl.BlockSpec(memory_space=pl.ANY),
        scratch_shapes=[
            pltpu.VMEM((LANES * OWN, LANES), F32),
            pltpu.VMEM((LANES + 2, OWN, LANES), BF16),
            pltpu.VMEM((LANES, LANES), F32),
            pltpu.VMEM((GROUP, BLOCK, LANES), F32),
            pltpu.VMEM((GROUP, BLOCK, LANES), F32),
            pltpu.VMEM((2, GROUP, OWN, LANES), BF16),
            pltpu.VMEM((2, SPEC, LANES), BF16),
            pltpu.VMEM((BLOCK + 2, SPEC, LANES), BF16),
            pltpu.VMEM((2, BLOCK + 2, SPEC, LANES), F32),
            pltpu.VMEM((STEPS * 64, LANES), F32),
            pltpu.VMEM((STEPS - 1, CHUNKS, 2, 64, LANES), BF16),
            pltpu.VMEM((STEPS, CHUNKS, 2, 64, LANES), BF16),
            pltpu.VMEM((STEPS - 1, 2, SPEC, LANES), BF16),
            pltpu.VMEM((STEPS - 1, 2, SPEC, LANES), BF16),
            pltpu.VMEM((SPEC, 2 * LANES), BF16),
            pltpu.VMEM((2 * SPEC, 2 * LANES), BF16),
            pltpu.VMEM((BLOCK, SPEC, LANES), BF16),
            dma((2, GROUP)), dma((2,)), dma((GROUP,)), dma(()), dma((2, GROUP)), dma((2,)),
            dma((STEPS - 1, CHUNKS, 2)), dma((STEPS - 1, CHUNKS, 2)), dma((STEPS - 1, 2)), dma((STEPS - 1, 2)),
            dma((CHUNKS, GROUP)), dma(()),
        ],
        compiler_params=pltpu.CompilerParams(collective_id=0, has_side_effects=True, vmem_limit_bytes=48 * 2**20),
        name="transport",
    )(tracers, fluxes, weight_in, weight_out)
    return pl.pallas_call(
        turn_back,
        out_shape=jax.ShapeDtypeStruct((OWN, 16, 8, LANES), F32),
        in_specs=[vmem],
        out_specs=vmem,
        scratch_shapes=[pltpu.VMEM((LANES * OWN, LANES), F32)],
        name="turn_back",
    )(back)


def solution(mesh):
    placed = (P("species", None, "tile", None), P(None, None, "species", "tile", None), P(), P())
    return jax.shard_map(
        per_device,
        mesh=mesh,
        in_specs=placed,
        out_specs=P("species", None, "tile", None),
        check_vma=False,
    )
```

time: 285 us -> 80.3 us (0.28)
  the two profiles are of different devices: /device:TPU:2 before, /device:TPU:1 now
where the time goes in v1:
time: 80.3 us; the launch traced here: 80.1 us
  Pallas kernels  75.3 us (94%)
  local copies, waits for them, and re-layouts  4.71 us (6%)
    pallas_call x1, Pallas kernels, per_device(): pl.pallas_call(transport, out_shape=jax.ShapeDtypeStruct((LANES, OWN, LAN...  71.5 us
    unnamed x10, local copies, waits for them, and re-layouts  4.71 us
    pallas_call x1, Pallas kernels, per_device(): pl.pallas_call(turn_back, out_shape=jax.ShapeDtypeStruct((OWN, 16, 8, LAN...  3.78 us

profile of v1, /device:TPU:1, one launch (start us, length us, event | category | flops | bytes accessed | tf_op | source)
XLA Modules:
  0.0 80.1 jit_solution(18430868374935377568)
XLA Ops:
  0.0 0.0 copy-start.1
  0.0 1.2 %copy-done.1 = f32[16,16,8,128]{3,2,1,0:T(8,128)S(1)} copy-done((f32[16,16,8,128]{3,2,1,0:T(8,128)S(1)}, f32[16,16,8,128]{3,2,1,0:T(8,128)}, u32[]{:S(2)}) %copy-start.1) | copy-done | bytes 1048600
  1.2 0.0 copy-start.2
  1.2 0.9 %copy-done.2 = bf16[512,256]{1,0:T(8,128)(2,1)S(1)} copy-done((bf16[512,256]{1,0:T(8,128)(2,1)S(1)}, bf16[512,256]{1,0:T(8,128)(2,1)}, u32[]{:S(2)}) %copy-start.2) | copy-done | bytes 262168
  2.2 0.0 copy-start.3
  2.2 0.9 %copy-done.3 = bf16[256,512]{1,0:T(8,128)(2,1)S(1)} copy-done((bf16[256,512]{1,0:T(8,128)(2,1)S(1)}, bf16[256,512]{1,0:T(8,128)(2,1)}, u32[]{:S(2)}) %copy-start.3) | copy-done | bytes 262168
  3.1 0.0 copy-start.4
  3.1 0.8 copy-done.4
  3.9 71.5 %transport.1.back = bf16[128,16,128]{2,1,0:T(8,128)(2,1)S(1)} custom-call(f32[16,16,8,128]{3,2,1,0:T(8,128)S(1)} %copy-done.1, f32[4,3,1,8,128]{4,3,2,1,0:T(8,128)S(1)} %copy-done.4, bf16[512,256]{1,0:T(8,128)(2,1)S(1)} %copy-done.2, bf16[256,512]{1,0:T(8,128)(2,1)S(1)} %copy-done.3), custom_call_target="tpu_custom_call" | custom-call | tf_op jit(solution)/shard_map/transport/pallas_call | solution.py:430
  75.5 0.0 copy-start
  75.5 0.8 copy-done
  76.3 3.8 %turn_back.1 = f32[16,16,8,128]{3,2,1,0:T(8,128)} custom-call(bf16[128,16,128]{2,1,0:T(8,128)(2,1)} %copy-done), custom_call_target="tpu_custom_call" | custom-call | tf_op jit(solution)/shard_map/turn_back/pallas_call | solution.py:460
Async XLA Ops:
  0.0 1.2 %copy-start.1 = (f32[16,16,8,128]{3,2,1,0:T(8,128)S(1)}, f32[16,16,8,128]{3,2,1,0:T(8,128)}, u32[]{:S(2)}) copy-start(f32[16,16,8,128]{3,2,1,0:T(8,128)} %tracers.1) | copy-start | bytes 3145732
  1.2 0.9 %copy-start.2 = (bf16[512,256]{1,0:T(8,128)(2,1)S(1)}, bf16[512,256]{1,0:T(8,128)(2,1)}, u32[]{:S(2)}) copy-start(bf16[512,256]{1,0:T(8,128)(2,1)} %weight_in.1) | copy-start | bytes 786436
  2.2 0.9 %copy-start.3 = (bf16[256,512]{1,0:T(8,128)(2,1)S(1)}, bf16[256,512]{1,0:T(8,128)(2,1)}, u32[]{:S(2)}) copy-start(bf16[256,512]{1,0:T(8,128)(2,1)} %weight_out.1) | copy-start | bytes 786436
  3.1 0.8 copy-start.4
  75.5 0.8 copy-start

commit v2 on v0

v2 whole, which is shorter than its diff:
```python
import jax
import jax.numpy as jnp
from jax import lax
from jax.experimental import pallas as pl
from jax.experimental.pallas import tpu as pltpu
from jax.sharding import PartitionSpec as P

STEPS = 4
GROUP = 16
TILES = 16
LANES = 128
PAIR = 2 * LANES
SPEC = 256
HID = 512
OWN = 16
BLOCK = 8
CHUNKS = 4
ORDER = (0, 3, 1, 2)
F32 = jnp.float32
BF16 = jnp.bfloat16
MESH = pl.DeviceIdType.MESH


def device_of(block):
    place = block // 2
    half = place // 4
    row = jnp.where(half == 0, place, 7 - place)
    return 4 * row + 2 * half + block % 2


def block_of(device):
    row = device // 4
    half = (device // 2) % 2
    place = jnp.where(half == 0, row, 7 - row)
    return 2 * place + device % 2


def transport(
    tracers_hbm, fluxes_hbm, weight_in_hbm, weight_out_hbm, out,
    tracers, fluxes, weight_in, weight_out, turned, sent, flux_out, flux_in, beyond_out, beyond_in,
    narrow, master, coeff, band, xs_out, xs_in, ys_in, hidden, back,
    load, flux_send, flux_recv, beyond_sem, main_send, main_recv,
    x_send, x_recv, y_send, y_recv, back_send, back_recv,
):
    spec = lax.axis_index("species")
    tile = lax.axis_index("tile")
    block = block_of(spec)
    right_tile = lax.rem(tile + 1, TILES)
    left_tile = lax.rem(tile + TILES - 1, TILES)
    upper = device_of(lax.rem(block + 1, GROUP))
    lower = device_of(lax.rem(block + GROUP - 1, GROUP))
    mine = pl.ds(pl.multiple_of(spec * OWN, OWN), OWN)

    loads = [
        pltpu.make_async_copy(fluxes_hbm, fluxes, load.at[0]),
        pltpu.make_async_copy(tracers_hbm, tracers, load.at[1]),
        pltpu.make_async_copy(weight_in_hbm, weight_in, load.at[2]),
        pltpu.make_async_copy(weight_out_hbm, weight_out, load.at[3]),
    ]
    for copy in loads:
        copy.start()

    barrier = pltpu.get_barrier_semaphore()

    def greet(k, carry):
        pl.semaphore_signal(
            barrier, inc=1, device_id=(lax.rem(spec + k, GROUP), tile), device_id_type=MESH
        )
        return carry

    lax.fori_loop(1, GROUP, greet, 0)
    for side_tile in (left_tile, right_tile):
        pl.semaphore_signal(barrier, inc=1, device_id=(spec, side_tile), device_id_type=MESH)

    loads[0].wait()
    rows = []
    for step in range(STEPS):
        along_y = fluxes[step, 1, 0]
        rows += [fluxes[step, 0, 0], along_y, fluxes[step, 2, 0], pltpu.roll(along_y, LANES - 1, 1)]
    flux_turned = jnp.concatenate(rows, 0).T
    for to in range(GROUP):
        flux_out[to] = flux_turned[to * BLOCK:(to + 1) * BLOCK].astype(BF16)

    loads[1].wait()

    def turn(part, carry):
        for i in range(4):
            own = part * 4 + i
            turned[pl.ds(own, LANES, stride=OWN), :] = tracers[own].reshape(LANES, LANES).T
        return carry

    lax.fori_loop(0, OWN // 4, turn, 0)

    def narrowed(y, carry):
        for yy in range(2):
            sent[y, :, yy * LANES:(yy + 1) * LANES] = turned[
                pl.ds(pl.multiple_of((2 * y + yy) * OWN, OWN), OWN), :
            ].astype(BF16)
        return carry

    lax.fori_loop(0, LANES // 2, narrowed, 0, unroll=8)

    pl.semaphore_wait(barrier, GROUP + 1)

    def flux_copy(k):
        peer = lax.rem(spec + k, GROUP)
        return pltpu.make_async_remote_copy(
            src_ref=flux_out.at[block_of(peer)],
            dst_ref=flux_in.at[spec],
            send_sem=flux_send.at[k],
            recv_sem=flux_recv,
            device_id=(peer, tile),
            device_id_type=MESH,
        )

    def main_copy(chunk, k):
        peer = lax.rem(spec + k, GROUP)
        return pltpu.make_async_remote_copy(
            src_ref=sent.at[block_of(peer) * CHUNKS + chunk],
            dst_ref=narrow.at[0, chunk, mine],
            send_sem=main_send.at[chunk, k],
            recv_sem=main_recv.at[chunk],
            device_id=(peer, tile),
            device_id_type=MESH,
        )

    pltpu.make_async_copy(flux_out.at[block], flux_in.at[spec], flux_recv).start()

    def send_flux(k, carry):
        flux_copy(k).start()
        return carry

    lax.fori_loop(1, GROUP, send_flux, 0)
    for chunk in ORDER:
        pltpu.make_async_copy(
            sent.at[block * CHUNKS + chunk], narrow.at[0, chunk, mine], main_recv.at[chunk]
        ).start()

        def send_main(k, carry, chunk=chunk):
            main_copy(chunk, k).start()
            return carry

        lax.fori_loop(1, GROUP, send_main, 0)

    loads[2].wait()
    loads[3].wait()
    weight_in[...] = weight_in[...] * jnp.asarray(0.5, BF16)
    weight_out[...] = weight_out[...] * jnp.asarray(0.5, BF16)

    lane = lax.broadcasted_iota(jnp.int32, (1, LANES), 1)
    at_x = lane % 8
    at_z = lane // 8

    pltpu.make_async_copy(flux_in, flux_in, flux_recv).wait()
    beyond_copy = pltpu.make_async_remote_copy(
        src_ref=beyond_out,
        dst_ref=beyond_in,
        send_sem=beyond_sem.at[0],
        recv_sem=beyond_sem.at[1],
        device_id=(spec, left_tile),
        device_id_type=MESH,
    )
    pieces = [flux_in[level].astype(F32) for level in range(16)]

    def field_of(step, field):
        value = jnp.zeros((BLOCK, LANES), F32)
        for level in range(16):
            shift = (level * 8 - (step * 4 + field) * 8) % LANES
            value = jnp.where(at_z == level, pltpu.roll(pieces[level], shift, 1) if shift else pieces[level], value)
        return value

    for step in range(STEPS):
        beyond_out[step] = jnp.where((at_x == 0) & (tile == 0), 0.0, field_of(step, 0))
    beyond_copy.start()
    others = [[field_of(step, field) for field in (1, 2, 3)] for step in range(STEPS)]
    beyond_copy.wait_recv()
    for step in range(STEPS):
        flux_x = beyond_out[step]
        flux_y, flux_z, flux_y_up = others[step]
        beyond = jnp.where(tile == TILES - 1, 0.0, pltpu.roll(beyond_in[step], 7, 1))
        flux_z = jnp.where(at_z == 0, 0.0, flux_z)
        flux_x_up = jnp.where(at_x == 7, beyond, pltpu.roll(flux_x, LANES - 1, 1))
        flux_z_up = pltpu.roll(flux_z, LANES - 8, 1)
        lows = [jnp.minimum(f, 0.0) for f in (flux_x, flux_y, flux_z)]
        highs = [jnp.maximum(f, 0.0) for f in (flux_x_up, flux_y_up, flux_z_up)]
        west, east = jnp.maximum(flux_x, 0.0), -jnp.minimum(flux_x_up, 0.0)
        terms = [
            (lows[0] - highs[0]) + (lows[1] - highs[1]) + (lows[2] - highs[2]),
            jnp.where(at_x == 0, 0.0, west),
            jnp.where(at_x == 7, 0.0, east),
            jnp.maximum(flux_z, 0.0),
            -jnp.minimum(flux_z_up, 0.0),
            jnp.maximum(flux_y, 0.0),
            -jnp.minimum(flux_y_up, 0.0),
            jnp.where(at_x == 0, west, jnp.where(at_x == 7, east, 0.0)),
        ]
        for which, term in enumerate(terms):
            coeff[pl.ds(step * 64 + which, BLOCK, stride=8), :] = term

    def bands(part, carry):
        at = pl.multiple_of((part % 8) * 16, 16)
        step = part // 8
        away = lax.broadcasted_iota(jnp.int32, (16, LANES), 1) - (
            lax.broadcasted_iota(jnp.int32, (16, LANES), 0) + at
        )
        masks = [away == d for d in (0, 1, -1, 8, -8)]
        for chunk in range(CHUNKS):
            for yy in range(2):
                table = coeff[pl.ds(pl.multiple_of((step * BLOCK + 2 * chunk + yy) * 8, 8), 8), :]
                value = jnp.zeros((16, LANES), F32)
                for i in range(5):
                    value = jnp.where(masks[i], table[i:i + 1], value)
                cross = jnp.where(masks[0], table[6:7] if yy == 0 else table[5:6], 0.0)
                lanes = slice(yy * LANES, (yy + 1) * LANES)
                band[step, chunk, pl.ds(yy * LANES + at, 16), lanes] = value.astype(BF16)
                band[step, chunk, pl.ds((1 - yy) * LANES + at, 16), lanes] = cross.astype(BF16)
        return carry

    lax.fori_loop(0, 8 * STEPS, bands, 0)

    def x_copy(step, chunk, side):
        return pltpu.make_async_remote_copy(
            src_ref=xs_out.at[step, chunk, side],
            dst_ref=xs_in.at[step, chunk, side],
            send_sem=x_send.at[step, chunk, side],
            recv_sem=x_recv.at[step, chunk, side],
            device_id=(spec, right_tile if side == 0 else left_tile),
            device_id_type=MESH,
        )

    def y_copy(step, side):
        return pltpu.make_async_remote_copy(
            src_ref=narrow.at[step, CHUNKS - 1 if side == 0 else 0, :, pl.ds(LANES if side == 0 else 0, LANES)],
            dst_ref=ys_in.at[step, side],
            send_sem=y_send.at[step, side],
            recv_sem=y_recv.at[step, side],
            device_id=(upper if side == 0 else lower, tile),
            device_id_type=MESH,
        )

    def publish(step, chunk):
        if chunk == 0:
            y_copy(step, 1).start()
        if chunk == CHUNKS - 1:
            y_copy(step, 0).start()
        for off in range(0, 64, 16):
            high = jnp.zeros((16, LANES), F32)
            low = jnp.zeros((16, LANES), F32)
            for q in range(4):
                for yy in range(2):
                    slot = 2 * q + yy
                    value = master[chunk, q * 64 + off:q * 64 + off + 16, yy * LANES:(yy + 1) * LANES]
                    high = jnp.where(at_x == slot, pltpu.roll(value, (slot - 7) % LANES, 1) if slot < 7 else value, high)
                    low = jnp.where(at_x == slot, pltpu.roll(value, slot, 1) if slot else value, low)
            xs_out[step, chunk, 0, off:off + 16] = high.astype(BF16)
            xs_out[step, chunk, 1, off:off + 16] = low.astype(BF16)
        x_copy(step, chunk, 0).start()
        x_copy(step, chunk, 1).start()

    for chunk in ORDER:
        pltpu.make_async_copy(narrow.at[0, chunk], narrow.at[0, chunk], main_recv.at[chunk]).wait()
        master[chunk] = narrow[0, chunk].astype(F32)
        publish(0, chunk)

    def back_copy(chunk, k):
        peer = lax.rem(spec + k, GROUP)
        return pltpu.make_async_remote_copy(
            src_ref=narrow.at[STEPS, chunk, pl.ds(pl.multiple_of(peer * OWN, OWN), OWN)],
            dst_ref=back.at[chunk, block],
            send_sem=back_send.at[chunk, k],
            recv_sem=back_recv.at[chunk],
            device_id=(peer, tile),
            device_id_type=MESH,
        )

    def do_chunk(step, chunk):
        x_copy(step, chunk, 0).wait_recv()
        x_copy(step, chunk, 1).wait_recv()
        if chunk == 0:
            y_copy(step, 0).wait_recv()
        if chunk == CHUNKS - 1:
            y_copy(step, 1).wait_recv()

        inner = jnp.dot(narrow[step, chunk], band[step, chunk], preferred_element_type=F32)
        tables = [
            coeff[pl.ds(pl.multiple_of((step * BLOCK + 2 * chunk + yy) * 8, 8), 8), :] for yy in range(2)
        ]
        for off in range(0, 64, 32):
            halo_l = xs_in[step, chunk, 0, off:off + 32].astype(F32)
            halo_r = xs_in[step, chunk, 1, off:off + 32].astype(F32)
            for q in range(4):
                for yy in range(2):
                    slot = 2 * q + yy
                    at = slice(off + q * 64, off + q * 64 + 32)
                    lanes = slice(yy * LANES, (yy + 1) * LANES)
                    if yy == 0:
                        outer = ys_in[step, 0, at] if chunk == 0 else narrow[step, chunk - 1, at, LANES:]
                        k_outer = tables[0][5:6]
                    else:
                        outer = ys_in[step, 1, at] if chunk == CHUNKS - 1 else narrow[step, chunk + 1, at, :LANES]
                        k_outer = tables[1][6:7]
                    from_l = pltpu.roll(halo_l, LANES - slot, 1) if slot else halo_l
                    from_r = pltpu.roll(halo_r, 7 - slot, 1) if slot < 7 else halo_r
                    new = master[chunk, at, lanes] + inner[at, lanes] + k_outer * outer.astype(F32)
                    new += tables[yy][7:8] * jnp.where(at_x == 0, from_l, from_r)
                    master[chunk, at, lanes] = new
                    narrow[step + 1, chunk, at, lanes] = new.astype(BF16)

        cells = narrow[step + 1, chunk]
        for part in range(4):
            rows_at = slice(part * LANES, (part + 1) * LANES)
            pre = jnp.dot(weight_in[rows_at], cells, preferred_element_type=F32)
            hidden[rows_at] = (pre + pre * jnp.tanh(pre)).astype(BF16)
        after = master[chunk] + jnp.dot(weight_out[...], hidden[...], preferred_element_type=F32)
        master[chunk] = after
        narrow[step + 1, chunk] = after.astype(BF16)

        @pl.when(step < STEPS - 1)
        def _():
            publish(step + 1, chunk)

        @pl.when(step == STEPS - 1)
        def _():
            pltpu.make_async_copy(narrow.at[STEPS, chunk, mine], back.at[chunk, block], back_recv.at[chunk]).start()

            def send_back(k, carry):
                back_copy(chunk, k).start()
                return carry

            lax.fori_loop(1, GROUP, send_back, 0)

    def do_step(step, carry):
        for chunk in ORDER:
            do_chunk(step, chunk)
        return carry

    lax.fori_loop(0, STEPS, do_step, 0)

    def sent_out(k, carry):
        flux_copy(k).wait_send()
        for chunk in range(CHUNKS):
            main_copy(chunk, k).wait_send()
        return carry

    lax.fori_loop(1, GROUP, sent_out, 0)
    beyond_copy.wait_send()

    def halos_out(step, carry):
        for side in range(2):
            y_copy(step, side).wait_send()
            for chunk in range(CHUNKS):
                x_copy(step, chunk, side).wait_send()
        return carry

    lax.fori_loop(0, STEPS, halos_out, 0)

    for chunk in ORDER:
        pltpu.make_async_copy(back.at[chunk], back.at[chunk], back_recv.at[chunk]).wait()

        def widen(of, carry, chunk=chunk):
            for yy in range(2):
                y = of * BLOCK + 2 * chunk + yy
                turned[pl.ds(pl.multiple_of(y * OWN, OWN), OWN), :] = back[
                    chunk, of, :, yy * LANES:(yy + 1) * LANES
                ].astype(F32)
            return carry

        lax.fori_loop(0, GROUP, widen, 0, unroll=4)

    def turn_back(part, carry):
        for i in range(4):
            own = part * 4 + i
            out[own] = turned[pl.ds(own, LANES, stride=OWN), :].T.reshape(16, 8, LANES)
        return carry

    lax.fori_loop(0, OWN // 4, turn_back, 0)

    def back_out(k, carry):
        for chunk in range(CHUNKS):
            back_copy(chunk, k).wait_send()
        return carry

    lax.fori_loop(1, GROUP, back_out, 0)


def per_device(tracers, fluxes, weight_in, weight_out):
    dma = pltpu.SemaphoreType.DMA
    return pl.pallas_call(
        transport,
        out_shape=jax.ShapeDtypeStruct(tracers.shape, F32),
        in_specs=[pl.BlockSpec(memory_space=pltpu.HBM)] * 4,
        out_specs=pl.BlockSpec(memory_space=pltpu.VMEM),
        scratch_shapes=[
            pltpu.VMEM(tracers.shape, F32),
            pltpu.VMEM(fluxes.shape, F32),
            pltpu.VMEM((HID, SPEC), BF16),
            pltpu.VMEM((SPEC, HID), BF16),
            pltpu.VMEM((LANES * OWN, LANES), F32),
            pltpu.VMEM((LANES // 2, OWN, PAIR), BF16),
            pltpu.VMEM((GROUP, BLOCK, LANES), BF16),
            pltpu.VMEM((GROUP, BLOCK, LANES), BF16),
            pltpu.VMEM((STEPS, BLOCK, LANES), F32),
            pltpu.VMEM((STEPS, BLOCK, LANES), F32),
            pltpu.VMEM((STEPS + 1, CHUNKS, SPEC, PAIR), BF16),
            pltpu.VMEM((CHUNKS, SPEC, PAIR), F32),
            pltpu.VMEM((STEPS * 64, LANES), F32),
            pltpu.VMEM((STEPS, CHUNKS, PAIR, PAIR), BF16),
            pltpu.VMEM((STEPS, CHUNKS, 2, 64, LANES), BF16),
            pltpu.VMEM((STEPS, CHUNKS, 2, 64, LANES), BF16),
            pltpu.VMEM((STEPS, 2, SPEC, LANES), BF16),
            pltpu.VMEM((HID, PAIR), BF16),
            pltpu.VMEM((CHUNKS, GROUP, OWN, PAIR), BF16),
            dma((4,)), dma((GROUP,)), dma(()), dma((2,)), dma((CHUNKS, GROUP)), dma((CHUNKS,)),
            dma((STEPS, CHUNKS, 2)), dma((STEPS, CHUNKS, 2)), dma((STEPS, 2)), dma((STEPS, 2)),
            dma((CHUNKS, GROUP)), dma((CHUNKS,)),
        ],
        compiler_params=pltpu.CompilerParams(collective_id=0, has_side_effects=True, vmem_limit_bytes=67043328),
        name="transport",
    )(tracers, fluxes, weight_in, weight_out)


def solution(mesh):
    placed = (P("species", None, "tile", None), P(None, None, "species", "tile", None), P(), P())
    return jax.shard_map(
        per_device,
        mesh=mesh,
        in_specs=placed,
        out_specs=P("species", None, "tile", None),
        check_vma=False,
    )
```

time: 285 us -> 58.6 us (0.21)
  the two profiles are of different devices: /device:TPU:2 before, /device:TPU:1 now
where the time goes in v2:
time: 58.6 us; the launch traced here: 58.4 us
  Pallas kernels  56.1 us (96%)
  local copies, waits for them, and re-layouts  2.3 us (4%)
    pallas_call x1, Pallas kernels, per_device(): pl.pallas_call(transport, out_shape=jax.ShapeDtypeStruct(tracers.shape, F...  56.1 us
    unnamed x1, local copies, waits for them, and re-layouts  2.3 us

profile of v2, /device:TPU:1, one launch (start us, length us, event | category | flops | bytes accessed | tf_op | source)
XLA Modules:
  0.0 58.4 jit_solution(4009038155509735795)
XLA Ops:
  0.0 56.1 %transport.1 = f32[16,16,8,128]{3,2,1,0:T(8,128)} custom-call(f32[16,16,8,128]{3,2,1,0:T(8,128)} %tracers_hbm.1, f32[4,3,1,8,128]{4,3,2,1,0:T(8,128)} %fluxes_hbm.1, bf16[512,256]{1,0:T(8,128)(2,1)} %weight_in_hbm.1, bf16[256,512]{1,0:T(8,128)(2,1)} %weight_out_hbm.1), custom_call_target="tpu_custom_call" | custom-call | tf_op jit(solution)/shard_map/transport/pallas_call | solution.py:388
  56.1 2.3 %copy.6 = f32[16,16,8,128]{3,2,1,0:T(8,128)} copy(f32[16,16,8,128]{3,2,1,0:T(8,128)} %transport.1) | data formatting | bytes 2097152

commit v3 on v2

--- a/solution.py
+++ b/solution.py
@@ -16,6 +16,7 @@
 BLOCK = 8
 CHUNKS = 4
 ORDER = (0, 3, 1, 2)
+PEERS = (8, 4, 12, 2, 9, 5, 13, 3, 10, 6, 14, 1, 11, 7, 15)
 F32 = jnp.float32
 BF16 = jnp.bfloat16
 MESH = pl.DeviceIdType.MESH
@@ -36,9 +37,9 @@
 
 
 def transport(
-    tracers_hbm, fluxes_hbm, weight_in_hbm, weight_out_hbm, out,
+    tracers_hbm, fluxes_hbm, weight_in_hbm, weight_out_hbm, back,
     tracers, fluxes, weight_in, weight_out, turned, sent, flux_out, flux_in, beyond_out, beyond_in,
-    narrow, master, coeff, band, xs_out, xs_in, ys_in, hidden, back,
+    narrow, master, coeff, band, xs_out, xs_in, ys_in, hidden,
     load, flux_send, flux_recv, beyond_sem, main_send, main_recv,
     x_send, x_recv, y_send, y_recv, back_send, back_recv,
 ):
@@ -53,10 +54,14 @@
 
     loads = [
         pltpu.make_async_copy(fluxes_hbm, fluxes, load.at[0]),
-        pltpu.make_async_copy(tracers_hbm, tracers, load.at[1]),
-        pltpu.make_async_copy(weight_in_hbm, weight_in, load.at[2]),
-        pltpu.make_async_copy(weight_out_hbm, weight_out, load.at[3]),
+        pltpu.make_async_copy(weight_in_hbm, weight_in, load.at[1]),
+        pltpu.make_async_copy(weight_out_hbm, weight_out, load.at[2]),
     ]
+    quarters = [
+        pltpu.make_async_copy(tracers_hbm.at[pl.ds(4 * i, 4)], tracers.at[pl.ds(4 * i, 4)], load.at[3 + i])
+        for i in range(4)
+    ]
+    loads = loads[:1] + quarters + loads[1:]
     for copy in loads:
         copy.start()
 
@@ -69,8 +74,19 @@
         return carry
 
     lax.fori_loop(1, GROUP, greet, 0)
-    for side_tile in (left_tile, right_tile):
-        pl.semaphore_signal(barrier, inc=1, device_id=(spec, side_tile), device_id_type=MESH)
+    has_side = (tile > 0, tile < TILES - 1)
+    side_tiles = (left_tile, right_tile)
+    for side in range(2):
+
+        @pl.when(has_side[side])
+        def _(side=side):
+            pl.semaphore_signal(barrier, inc=1, device_id=(spec, side_tiles[side]), device_id_type=MESH)
+
+        @pl.when(jnp.logical_not(has_side[side]))
+        def _(side=side):
+            xs_in[:, :, side] = jnp.zeros((STEPS, CHUNKS, 64, LANES), BF16)
+            if side == 1:
+                beyond_in[...] = jnp.zeros((STEPS, BLOCK, LANES), F32)
 
     loads[0].wait()
     rows = []
@@ -81,15 +97,11 @@
     for to in range(GROUP):
         flux_out[to] = flux_turned[to * BLOCK:(to + 1) * BLOCK].astype(BF16)
 
-    loads[1].wait()
-
-    def turn(part, carry):
+    for part in range(4):
+        quarters[part].wait()
         for i in range(4):
             own = part * 4 + i
             turned[pl.ds(own, LANES, stride=OWN), :] = tracers[own].reshape(LANES, LANES).T
-        return carry
-
-    lax.fori_loop(0, OWN // 4, turn, 0)
 
     def narrowed(y, carry):
         for yy in range(2):
@@ -100,14 +112,14 @@
 
     lax.fori_loop(0, LANES // 2, narrowed, 0, unroll=8)
 
-    pl.semaphore_wait(barrier, GROUP + 1)
+    pl.semaphore_wait(barrier, GROUP - 1 + has_side[0].astype(jnp.int32) + has_side[1].astype(jnp.int32))
 
     def flux_copy(k):
         peer = lax.rem(spec + k, GROUP)
         return pltpu.make_async_remote_copy(
             src_ref=flux_out.at[block_of(peer)],
             dst_ref=flux_in.at[spec],
-            send_sem=flux_send.at[k],
+            send_sem=flux_send,
             recv_sem=flux_recv,
             device_id=(peer, tile),
             device_id_type=MESH,
@@ -118,7 +130,7 @@
         return pltpu.make_async_remote_copy(
             src_ref=sent.at[block_of(peer) * CHUNKS + chunk],
             dst_ref=narrow.at[0, chunk, mine],
-            send_sem=main_send.at[chunk, k],
+            send_sem=main_send,
             recv_sem=main_recv.at[chunk],
             device_id=(peer, tile),
             device_id_type=MESH,
@@ -126,24 +138,17 @@
 
     pltpu.make_async_copy(flux_out.at[block], flux_in.at[spec], flux_recv).start()
 
-    def send_flux(k, carry):
+    for k in PEERS:
         flux_copy(k).start()
-        return carry
-
-    lax.fori_loop(1, GROUP, send_flux, 0)
     for chunk in ORDER:
         pltpu.make_async_copy(
             sent.at[block * CHUNKS + chunk], narrow.at[0, chunk, mine], main_recv.at[chunk]
         ).start()
-
-        def send_main(k, carry, chunk=chunk):
+        for k in PEERS:
             main_copy(chunk, k).start()
-            return carry
-
-        lax.fori_loop(1, GROUP, send_main, 0)
-
-    loads[2].wait()
-    loads[3].wait()
+
+    loads[5].wait()
+    loads[6].wait()
     weight_in[...] = weight_in[...] * jnp.asarray(0.5, BF16)
     weight_out[...] = weight_out[...] * jnp.asarray(0.5, BF16)
 
@@ -171,9 +176,17 @@
 
     for step in range(STEPS):
         beyond_out[step] = jnp.where((at_x == 0) & (tile == 0), 0.0, field_of(step, 0))
-    beyond_copy.start()
+
+    @pl.when(has_side[0])
+    def _():
+        beyond_copy.start()
+
     others = [[field_of(step, field) for field in (1, 2, 3)] for step in range(STEPS)]
-    beyond_copy.wait_recv()
+
+    @pl.when(has_side[1])
+    def _():
+        beyond_copy.wait_recv()
+
     for step in range(STEPS):
         flux_x = beyond_out[step]
         flux_y, flux_z, flux_y_up = others[step]
@@ -220,10 +233,10 @@
 
     def x_copy(step, chunk, side):
         return pltpu.make_async_remote_copy(
-            src_ref=xs_out.at[step, chunk, side],
+            src_ref=xs_out.at[side, step, chunk],
             dst_ref=xs_in.at[step, chunk, side],
-            send_sem=x_send.at[step, chunk, side],
-            recv_sem=x_recv.at[step, chunk, side],
+            send_sem=x_send.at[side],
+            recv_sem=x_recv.at[step, chunk],
             device_id=(spec, right_tile if side == 0 else left_tile),
             device_id_type=MESH,
         )
@@ -232,7 +245,7 @@
         return pltpu.make_async_remote_copy(
             src_ref=narrow.at[step, CHUNKS - 1 if side == 0 else 0, :, pl.ds(LANES if side == 0 else 0, LANES)],
             dst_ref=ys_in.at[step, side],
-            send_sem=y_send.at[step, side],
+            send_sem=y_send,
             recv_sem=y_recv.at[step, side],
             device_id=(upper if side == 0 else lower, tile),
             device_id_type=MESH,
@@ -252,10 +265,13 @@
                     value = master[chunk, q * 64 + off:q * 64 + off + 16, yy * LANES:(yy + 1) * LANES]
                     high = jnp.where(at_x == slot, pltpu.roll(value, (slot - 7) % LANES, 1) if slot < 7 else value, high)
                     low = jnp.where(at_x == slot, pltpu.roll(value, slot, 1) if slot else value, low)
-            xs_out[step, chunk, 0, off:off + 16] = high.astype(BF16)
-            xs_out[step, chunk, 1, off:off + 16] = low.astype(BF16)
-        x_copy(step, chunk, 0).start()
-        x_copy(step, chunk, 1).start()
+            xs_out[0, step, chunk, off:off + 16] = high.astype(BF16)
+            xs_out[1, step, chunk, off:off + 16] = low.astype(BF16)
+        for side in range(2):
+
+            @pl.when(has_side[1 - side])
+            def _(side=side):
+                x_copy(step, chunk, side).start()
 
     for chunk in ORDER:
         pltpu.make_async_copy(narrow.at[0, chunk], narrow.at[0, chunk], main_recv.at[chunk]).wait()
@@ -267,24 +283,44 @@
         return pltpu.make_async_remote_copy(
             src_ref=narrow.at[STEPS, chunk, pl.ds(pl.multiple_of(peer * OWN, OWN), OWN)],
             dst_ref=back.at[chunk, block],
-            send_sem=back_send.at[chunk, k],
+            send_sem=back_send,
             recv_sem=back_recv.at[chunk],
             device_id=(peer, tile),
             device_id_type=MESH,
         )
 
-    def do_chunk(step, chunk):
-        x_copy(step, chunk, 0).wait_recv()
-        x_copy(step, chunk, 1).wait_recv()
+    def table_of(step, chunk, yy):
+        return coeff[pl.ds(pl.multiple_of((step * BLOCK + 2 * chunk + yy) * 8, 8), 8), :]
+
+    def before_edges(step, chunk):
         if chunk == 0:
             y_copy(step, 0).wait_recv()
         if chunk == CHUNKS - 1:
             y_copy(step, 1).wait_recv()
-
         inner = jnp.dot(narrow[step, chunk], band[step, chunk], preferred_element_type=F32)
-        tables = [
-            coeff[pl.ds(pl.multiple_of((step * BLOCK + 2 * chunk + yy) * 8, 8), 8), :] for yy in range(2)
-        ]
+        for yy in range(2):
+            lanes = slice(yy * LANES, (yy + 1) * LANES)
+            if yy == 0:
+                outer = ys_in[step, 0] if chunk == 0 else narrow[step, chunk - 1, :, LANES:]
+            else:
+                outer = ys_in[step, 1] if chunk == CHUNKS - 1 else narrow[step, chunk + 1, :, :LANES]
+            k_outer = table_of(step, chunk, yy)[5 + yy:6 + yy]
+            master[chunk, :, lanes] += inner[:, lanes] + k_outer * outer.astype(F32)
+
+    def do_chunk(step, chunk):
+        both = has_side[0] & has_side[1]
+
+        @pl.when(both)
+        def _():
+            whole = xs_in.at[step, chunk]
+            pltpu.make_async_copy(whole, whole, x_recv.at[step, chunk]).wait()
+
+        @pl.when(jnp.logical_not(both))
+        def _():
+            one = xs_in.at[step, chunk, 0]
+            pltpu.make_async_copy(one, one, x_recv.at[step, chunk]).wait()
+
+        tables = [table_of(step, chunk, yy) for yy in range(2)]
         for off in range(0, 64, 32):
             halo_l = xs_in[step, chunk, 0, off:off + 32].astype(F32)
             halo_r = xs_in[step, chunk, 1, off:off + 32].astype(F32)
@@ -293,24 +329,15 @@
                     slot = 2 * q + yy
                     at = slice(off + q * 64, off + q * 64 + 32)
                     lanes = slice(yy * LANES, (yy + 1) * LANES)
-                    if yy == 0:
-                        outer = ys_in[step, 0, at] if chunk == 0 else narrow[step, chunk - 1, at, LANES:]
-                        k_outer = tables[0][5:6]
-                    else:
-                        outer = ys_in[step, 1, at] if chunk == CHUNKS - 1 else narrow[step, chunk + 1, at, :LANES]
-                        k_outer = tables[1][6:7]
                     from_l = pltpu.roll(halo_l, LANES - slot, 1) if slot else halo_l
                     from_r = pltpu.roll(halo_r, 7 - slot, 1) if slot < 7 else halo_r
-                    new = master[chunk, at, lanes] + inner[at, lanes] + k_outer * outer.astype(F32)
-                    new += tables[yy][7:8] * jnp.where(at_x == 0, from_l, from_r)
+                    new = master[chunk, at, lanes] + tables[yy][7:8] * jnp.where(at_x == 0, from_l, from_r)
                     master[chunk, at, lanes] = new
                     narrow[step + 1, chunk, at, lanes] = new.astype(BF16)
 
         cells = narrow[step + 1, chunk]
-        for part in range(4):
-            rows_at = slice(part * LANES, (part + 1) * LANES)
-            pre = jnp.dot(weight_in[rows_at], cells, preferred_element_type=F32)
-            hidden[rows_at] = (pre + pre * jnp.tanh(pre)).astype(BF16)
+        pre = jnp.dot(weight_in[...], cells, preferred_element_type=F32)
+        hidden[...] = (pre + pre * jnp.tanh(pre)).astype(BF16)
         after = master[chunk] + jnp.dot(weight_out[...], hidden[...], preferred_element_type=F32)
         master[chunk] = after
         narrow[step + 1, chunk] = after.astype(BF16)
@@ -322,74 +349,75 @@
         @pl.when(step == STEPS - 1)
         def _():
             pltpu.make_async_copy(narrow.at[STEPS, chunk, mine], back.at[chunk, block], back_recv.at[chunk]).start()
-
-            def send_back(k, carry):
+            for k in PEERS:
                 back_copy(chunk, k).start()
-                return carry
-
-            lax.fori_loop(1, GROUP, send_back, 0)
 
     def do_step(step, carry):
+        for chunk in (1, 2, 0, 3):
+            before_edges(step, chunk)
         for chunk in ORDER:
             do_chunk(step, chunk)
         return carry
 
     lax.fori_loop(0, STEPS, do_step, 0)
 
-    def sent_out(k, carry):
-        flux_copy(k).wait_send()
-        for chunk in range(CHUNKS):
-            main_copy(chunk, k).wait_send()
-        return carry
-
-    lax.fori_loop(1, GROUP, sent_out, 0)
-    beyond_copy.wait_send()
-
-    def halos_out(step, carry):
-        for side in range(2):
-            y_copy(step, side).wait_send()
-            for chunk in range(CHUNKS):
-                x_copy(step, chunk, side).wait_send()
-        return carry
-
-    lax.fori_loop(0, STEPS, halos_out, 0)
-
+    def drain(ref, sem):
+        pltpu.make_async_copy(ref, ref, sem).wait()
+
+    @pl.when(has_side[0])
+    def _():
+        beyond_copy.wait_send()
+
+    for side in range(2):
+
+        @pl.when(has_side[1 - side])
+        def _(side=side):
+            drain(xs_out.at[side], x_send.at[side])
+
+    drain(flux_out.at[pl.ds(0, GROUP - 1)], flux_send)
+    drain(sent.at[pl.ds(0, (GROUP - 1) * CHUNKS)], main_send)
+    drain(ys_in, y_send)
     for chunk in ORDER:
-        pltpu.make_async_copy(back.at[chunk], back.at[chunk], back_recv.at[chunk]).wait()
+        drain(back.at[chunk], back_recv.at[chunk])
+    drain(sent.at[pl.ds(0, (GROUP - 1) * CHUNKS)], back_send)
+
+
+def turn_back(back, out, part_in, wide, part_out, load, store):
+    loads = [pltpu.make_async_copy(back.at[chunk], part_in.at[chunk], load.at[chunk]) for chunk in range(CHUNKS)]
+    for copy in loads:
+        copy.start()
+    for chunk in range(CHUNKS):
+        loads[chunk].wait()
 
         def widen(of, carry, chunk=chunk):
             for yy in range(2):
                 y = of * BLOCK + 2 * chunk + yy
-                turned[pl.ds(pl.multiple_of(y * OWN, OWN), OWN), :] = back[
+                wide[pl.ds(pl.multiple_of(y * OWN, OWN), OWN), :] = part_in[
                     chunk, of, :, yy * LANES:(yy + 1) * LANES
                 ].astype(F32)
             return carry
 
         lax.fori_loop(0, GROUP, widen, 0, unroll=4)
-
-    def turn_back(part, carry):
+    stores = []
+    for part in range(4):
         for i in range(4):
             own = part * 4 + i
-            out[own] = turned[pl.ds(own, LANES, stride=OWN), :].T.reshape(16, 8, LANES)
-        return carry
-
-    lax.fori_loop(0, OWN // 4, turn_back, 0)
-
-    def back_out(k, carry):
-        for chunk in range(CHUNKS):
-            back_copy(chunk, k).wait_send()
-        return carry
-
-    lax.fori_loop(1, GROUP, back_out, 0)
+            part_out[own] = wide[pl.ds(own, LANES, stride=OWN), :].T.reshape(16, 8, LANES)
+        span = pl.ds(4 * part, 4)
+        stores.append(pltpu.make_async_copy(part_out.at[span], out.at[span], store.at[part]))
+        stores[-1].start()
+    for copy in stores:
+        copy.wait()
 
 
 def per_device(tracers, fluxes, weight_in, weight_out):
     dma = pltpu.SemaphoreType.DMA
-    return pl.pallas_call(
+    hbm = pl.BlockSpec(memory_space=pltpu.HBM)
+    back = pl.pallas_call(
         transport,
-        out_shape=jax.ShapeDtypeStruct(tracers.shape, F32),
-        in_specs=[pl.BlockSpec(memory_space=pltpu.HBM)] * 4,
-        out_specs=pl.BlockSpec(memory_space=pltpu.VMEM),
+        out_shape=jax.ShapeDtypeStruct((CHUNKS, GROUP, OWN, PAIR), BF16),
+        in_specs=[hbm] * 4,
+        out_specs=hbm,
         scratch_shapes=[
             pltpu.VMEM(tracers.shape, F32),
             pltpu.VMEM(fluxes.shape, F32),
@@ -405,18 +433,30 @@
             pltpu.VMEM((CHUNKS, SPEC, PAIR), F32),
             pltpu.VMEM((STEPS * 64, LANES), F32),
             pltpu.VMEM((STEPS, CHUNKS, PAIR, PAIR), BF16),
-            pltpu.VMEM((STEPS, CHUNKS, 2, 64, LANES), BF16),
+            pltpu.VMEM((2, STEPS, CHUNKS, 64, LANES), BF16),
             pltpu.VMEM((STEPS, CHUNKS, 2, 64, LANES), BF16),
             pltpu.VMEM((STEPS, 2, SPEC, LANES), BF16),
             pltpu.VMEM((HID, PAIR), BF16),
-            pltpu.VMEM((CHUNKS, GROUP, OWN, PAIR), BF16),
-            dma((4,)), dma((GROUP,)), dma(()), dma((2,)), dma((CHUNKS, GROUP)), dma((CHUNKS,)),
-            dma((STEPS, CHUNKS, 2)), dma((STEPS, CHUNKS, 2)), dma((STEPS, 2)), dma((STEPS, 2)),
-            dma((CHUNKS, GROUP)), dma((CHUNKS,)),
+            dma((7,)), dma(()), dma(()), dma((2,)), dma(()), dma((CHUNKS,)),
+            dma((2,)), dma((STEPS, CHUNKS)), dma(()), dma((STEPS, 2)), dma(()), dma((CHUNKS,)),
         ],
         compiler_params=pltpu.CompilerParams(collective_id=0, has_side_effects=True, vmem_limit_bytes=67043328),
         name="transport",
     )(tracers, fluxes, weight_in, weight_out)
+    return pl.pallas_call(
+        turn_back,
+        out_shape=jax.ShapeDtypeStruct(tracers.shape, F32),
+        in_specs=[hbm],
+        out_specs=hbm,
+        scratch_shapes=[
+            pltpu.VMEM((CHUNKS, GROUP, OWN, PAIR), BF16),
+            pltpu.VMEM((LANES * OWN, LANES), F32),
+            pltpu.VMEM(tracers.shape, F32),
+            dma((CHUNKS,)), dma((4,)),
+        ],
+        compiler_params=pltpu.CompilerParams(vmem_limit_bytes=67043328),
+        name="turn_back",
+    )(back)
 
 
 def solution(mesh):

time: 58.6 us -> 50.1 us (0.85)
  Pallas kernels: 56.1 us -> 50 us
  local copies, waits for them, and re-layouts: 2.3 us -> 0 us
    pallas_call x1 -> x2, Pallas kernels: 56.1 us -> 50 us  [the longest x1 47.7 us: per_device(): pl.pallas_call(transport, out_shape=jax.ShapeDtypeStruct((CHUNKS, GROUP,...]
    unnamed x1 -> x0, local copies, waits for them, and re-layouts: 2.3 us -> none
where the time goes in v3:
time: 50.1 us; the launch traced here: 50 us
  Pallas kernels  50 us (100%)
    pallas_call x1, Pallas kernels, per_device(): pl.pallas_call(transport, out_shape=jax.ShapeDtypeStruct((CHUNKS, GROUP,...  47.7 us
    pallas_call x1, Pallas kernels, per_device(): pl.pallas_call(turn_back, out_shape=jax.ShapeDtypeStruct(tracers.shape, F...  2.29 us

profile of v3, /device:TPU:1, one launch (start us, length us, event | category | flops | bytes accessed | tf_op | source)
XLA Modules:
  0.0 50.0 jit_solution(2256539534282260041)
XLA Ops:
  0.0 47.7 %transport.1.back = bf16[4,16,16,256]{3,2,1,0:T(8,128)(2,1)} custom-call(f32[16,16,8,128]{3,2,1,0:T(8,128)} %tracers_hbm.1, f32[4,3,1,8,128]{4,3,2,1,0:T(8,128)} %fluxes_hbm.1, bf16[512,256]{1,0:T(8,128)(2,1)} %weight_in_hbm.1, bf16[256,512]{1,0:T(8,128)(2,1)} %weight_out_hbm.1), custom_call_target="tpu_custom_call" | custom-call | tf_op jit(solution)/shard_map/transport/pallas_call | solution.py:416
  47.7 2.3 %turn_back.1 = f32[16,16,8,128]{3,2,1,0:T(8,128)} custom-call(bf16[4,16,16,256]{3,2,1,0:T(8,128)(2,1)} %transport.1.back), custom_call_target="tpu_custom_call" | custom-call | tf_op jit(solution)/shard_map/turn_back/pallas_call | solution.py:446

commit v4 on v3

--- a/solution.py
+++ b/solution.py
@@ -15,6 +15,7 @@
 OWN = 16
 BLOCK = 8
 CHUNKS = 4
+EDGE_ROWS = 128
 ORDER = (0, 3, 1, 2)
 PEERS = (8, 4, 12, 2, 9, 5, 13, 3, 10, 6, 14, 1, 11, 7, 15)
 F32 = jnp.float32
@@ -22,18 +23,8 @@
 MESH = pl.DeviceIdType.MESH
 
 
-def device_of(block):
-    place = block // 2
-    half = place // 4
-    row = jnp.where(half == 0, place, 7 - place)
-    return 4 * row + 2 * half + block % 2
-
-
 def block_of(device):
-    row = device // 4
-    half = (device // 2) % 2
-    place = jnp.where(half == 0, row, 7 - row)
-    return 2 * place + device % 2
+    return (device // 2) % 2 * 8 + device // 4 * 2 + device % 2
 
 
 def transport(
@@ -46,10 +37,32 @@
     spec = lax.axis_index("species")
     tile = lax.axis_index("tile")
     block = block_of(spec)
-    right_tile = lax.rem(tile + 1, TILES)
-    left_tile = lax.rem(tile + TILES - 1, TILES)
-    upper = device_of(lax.rem(block + 1, GROUP))
-    lower = device_of(lax.rem(block + GROUP - 1, GROUP))
+    half = block // 8
+    across = spec + 2 - 4 * half
+    left_device = (across, jnp.where(half == 1, tile, tile - 1))
+    right_device = (across, jnp.where(half == 0, tile, tile + 1))
+    part = block % 8
+
+    def along_y(rows_at):
+        return (rows_at // 2 * 4 + half * 2 + rows_at % 2, tile)
+
+    upper = along_y(lax.rem(part + 1, 8))
+    lower = along_y(lax.rem(part + 7, 8))
+    at_start = (tile == 0) & (half == 0)
+    at_end = (tile == TILES - 1) & (half == 1)
+    has_side = (jnp.logical_not(at_start), jnp.logical_not(at_end))
+    side_devices = (left_device, right_device)
+    lane = lax.broadcasted_iota(jnp.int32, (1, LANES), 1)
+    at_x = lane % 4
+    at_p = lane // 4 % 2
+    at_z = lane // 8
+
+    def halves(even, odd):
+        return (
+            jnp.where(at_p == 0, even, pltpu.roll(odd, 4, 1)),
+            jnp.where(at_p == 0, pltpu.roll(even, LANES - 4, 1), odd),
+        )
+
     mine = pl.ds(pl.multiple_of(spec * OWN, OWN), OWN)
 
     loads = [
@@ -74,28 +87,27 @@
         return carry
 
     lax.fori_loop(1, GROUP, greet, 0)
-    has_side = (tile > 0, tile < TILES - 1)
-    side_tiles = (left_tile, right_tile)
     for side in range(2):
 
         @pl.when(has_side[side])
         def _(side=side):
-            pl.semaphore_signal(barrier, inc=1, device_id=(spec, side_tiles[side]), device_id_type=MESH)
+            pl.semaphore_signal(barrier, inc=1, device_id=side_devices[side], device_id_type=MESH)
 
         @pl.when(jnp.logical_not(has_side[side]))
         def _(side=side):
-            xs_in[:, :, side] = jnp.zeros((STEPS, CHUNKS, 64, LANES), BF16)
+            xs_in[:, :, side] = jnp.zeros((STEPS, CHUNKS, EDGE_ROWS, LANES), BF16)
             if side == 1:
                 beyond_in[...] = jnp.zeros((STEPS, BLOCK, LANES), F32)
 
     loads[0].wait()
     rows = []
     for step in range(STEPS):
-        along_y = fluxes[step, 1, 0]
-        rows += [fluxes[step, 0, 0], along_y, fluxes[step, 2, 0], pltpu.roll(along_y, LANES - 1, 1)]
-    flux_turned = jnp.concatenate(rows, 0).T
+        flux_y = fluxes[step, 1, 0]
+        rows += [fluxes[step, 0, 0], flux_y, fluxes[step, 2, 0], pltpu.roll(flux_y, LANES - 1, 1)]
+    turned[:LANES] = jnp.concatenate(rows, 0).T
+    pairs = halves(turned[pl.ds(0, LANES // 2, stride=2), :], turned[pl.ds(1, LANES // 2, stride=2), :])
     for to in range(GROUP):
-        flux_out[to] = flux_turned[to * BLOCK:(to + 1) * BLOCK].astype(BF16)
+        flux_out[to] = pairs[to // 8][to % 8 * BLOCK:(to % 8 + 1) * BLOCK].astype(BF16)
 
     for part in range(4):
         quarters[part].wait()
@@ -103,14 +115,16 @@
             own = part * 4 + i
             turned[pl.ds(own, LANES, stride=OWN), :] = tracers[own].reshape(LANES, LANES).T
 
-    def narrowed(y, carry):
-        for yy in range(2):
-            sent[y, :, yy * LANES:(yy + 1) * LANES] = turned[
-                pl.ds(pl.multiple_of((2 * y + yy) * OWN, OWN), OWN), :
-            ].astype(BF16)
+    def narrowed(to, carry):
+        for chunk in range(CHUNKS):
+            for yy in range(2):
+                at = pl.multiple_of((to * 16 + chunk * 4 + yy * 2) * OWN, 2 * OWN)
+                both = halves(turned[pl.ds(at, OWN), :], turned[pl.ds(at + OWN, OWN), :])
+                for of in range(2):
+                    sent[of * 8 + to, chunk, :, yy * LANES:(yy + 1) * LANES] = both[of].astype(BF16)
         return carry
 
-    lax.fori_loop(0, LANES // 2, narrowed, 0, unroll=8)
+    lax.fori_loop(0, 8, narrowed, 0)
 
     pl.semaphore_wait(barrier, GROUP - 1 + has_side[0].astype(jnp.int32) + has_side[1].astype(jnp.int32))
 
@@ -128,7 +142,7 @@
     def main_copy(chunk, k):
         peer = lax.rem(spec + k, GROUP)
         return pltpu.make_async_remote_copy(
-            src_ref=sent.at[block_of(peer) * CHUNKS + chunk],
+            src_ref=sent.at[block_of(peer), chunk],
             dst_ref=narrow.at[0, chunk, mine],
             send_sem=main_send,
             recv_sem=main_recv.at[chunk],
@@ -142,7 +156,7 @@
         flux_copy(k).start()
     for chunk in ORDER:
         pltpu.make_async_copy(
-            sent.at[block * CHUNKS + chunk], narrow.at[0, chunk, mine], main_recv.at[chunk]
+            sent.at[block, chunk], narrow.at[0, chunk, mine], main_recv.at[chunk]
         ).start()
         for k in PEERS:
             main_copy(chunk, k).start()
@@ -151,10 +165,6 @@
     loads[6].wait()
     weight_in[...] = weight_in[...] * jnp.asarray(0.5, BF16)
     weight_out[...] = weight_out[...] * jnp.asarray(0.5, BF16)
-
-    lane = lax.broadcasted_iota(jnp.int32, (1, LANES), 1)
-    at_x = lane % 8
-    at_z = lane // 8
 
     pltpu.make_async_copy(flux_in, flux_in, flux_recv).wait()
     beyond_copy = pltpu.make_async_remote_copy(
@@ -162,7 +172,7 @@
         dst_ref=beyond_in,
         send_sem=beyond_sem.at[0],
         recv_sem=beyond_sem.at[1],
-        device_id=(spec, left_tile),
+        device_id=left_device,
         device_id_type=MESH,
     )
     pieces = [flux_in[level].astype(F32) for level in range(16)]
@@ -175,7 +185,7 @@
         return value
 
     for step in range(STEPS):
-        beyond_out[step] = jnp.where((at_x == 0) & (tile == 0), 0.0, field_of(step, 0))
+        beyond_out[step] = jnp.where((at_x == 0) & at_start, 0.0, field_of(step, 0))
 
     @pl.when(has_side[0])
     def _():
@@ -190,9 +200,9 @@
     for step in range(STEPS):
         flux_x = beyond_out[step]
         flux_y, flux_z, flux_y_up = others[step]
-        beyond = jnp.where(tile == TILES - 1, 0.0, pltpu.roll(beyond_in[step], 7, 1))
+        beyond = jnp.where(at_end, 0.0, pltpu.roll(beyond_in[step], 3, 1))
         flux_z = jnp.where(at_z == 0, 0.0, flux_z)
-        flux_x_up = jnp.where(at_x == 7, beyond, pltpu.roll(flux_x, LANES - 1, 1))
+        flux_x_up = jnp.where(at_x == 3, beyond, pltpu.roll(flux_x, LANES - 1, 1))
         flux_z_up = pltpu.roll(flux_z, LANES - 8, 1)
         lows = [jnp.minimum(f, 0.0) for f in (flux_x, flux_y, flux_z)]
         highs = [jnp.maximum(f, 0.0) for f in (flux_x_up, flux_y_up, flux_z_up)]
@@ -200,12 +210,12 @@
         terms = [
             (lows[0] - highs[0]) + (lows[1] - highs[1]) + (lows[2] - highs[2]),
             jnp.where(at_x == 0, 0.0, west),
-            jnp.where(at_x == 7, 0.0, east),
+            jnp.where(at_x == 3, 0.0, east),
             jnp.maximum(flux_z, 0.0),
             -jnp.minimum(flux_z_up, 0.0),
             jnp.maximum(flux_y, 0.0),
             -jnp.minimum(flux_y_up, 0.0),
-            jnp.where(at_x == 0, west, jnp.where(at_x == 7, east, 0.0)),
+            jnp.where(at_x == 0, west, jnp.where(at_x == 3, east, 0.0)),
         ]
         for which, term in enumerate(terms):
             coeff[pl.ds(step * 64 + which, BLOCK, stride=8), :] = term
@@ -216,14 +226,17 @@
         away = lax.broadcasted_iota(jnp.int32, (16, LANES), 1) - (
             lax.broadcasted_iota(jnp.int32, (16, LANES), 0) + at
         )
+        parity = lax.broadcasted_iota(jnp.int32, (16, LANES), 1) // 4 % 2
         masks = [away == d for d in (0, 1, -1, 8, -8)]
+        masks += [(away == 4) & (parity == 1), (away == -4) & (parity == 0)]
+        crossing = [(away == 4) & (parity == 1), (away == -4) & (parity == 0)]
         for chunk in range(CHUNKS):
             for yy in range(2):
                 table = coeff[pl.ds(pl.multiple_of((step * BLOCK + 2 * chunk + yy) * 8, 8), 8), :]
                 value = jnp.zeros((16, LANES), F32)
-                for i in range(5):
+                for i in range(7):
                     value = jnp.where(masks[i], table[i:i + 1], value)
-                cross = jnp.where(masks[0], table[6:7] if yy == 0 else table[5:6], 0.0)
+                cross = jnp.where(crossing[yy], table[6:7] if yy == 0 else table[5:6], 0.0)
                 lanes = slice(yy * LANES, (yy + 1) * LANES)
                 band[step, chunk, pl.ds(yy * LANES + at, 16), lanes] = value.astype(BF16)
                 band[step, chunk, pl.ds((1 - yy) * LANES + at, 16), lanes] = cross.astype(BF16)
@@ -237,7 +250,7 @@
             dst_ref=xs_in.at[step, chunk, side],
             send_sem=x_send.at[side],
             recv_sem=x_recv.at[step, chunk],
-            device_id=(spec, right_tile if side == 0 else left_tile),
+            device_id=side_devices[1 - side],
             device_id_type=MESH,
         )
 
@@ -247,7 +260,7 @@
             dst_ref=ys_in.at[step, side],
             send_sem=y_send,
             recv_sem=y_recv.at[step, side],
-            device_id=(upper if side == 0 else lower, tile),
+            device_id=upper if side == 0 else lower,
             device_id_type=MESH,
         )
 
@@ -256,14 +269,15 @@
             y_copy(step, 1).start()
         if chunk == CHUNKS - 1:
             y_copy(step, 0).start()
-        for off in range(0, 64, 16):
+        for off in range(0, EDGE_ROWS, 16):
             high = jnp.zeros((16, LANES), F32)
             low = jnp.zeros((16, LANES), F32)
-            for q in range(4):
+            for q in range(2):
                 for yy in range(2):
                     slot = 2 * q + yy
-                    value = master[chunk, q * 64 + off:q * 64 + off + 16, yy * LANES:(yy + 1) * LANES]
-                    high = jnp.where(at_x == slot, pltpu.roll(value, (slot - 7) % LANES, 1) if slot < 7 else value, high)
+                    at = q * EDGE_ROWS + off
+                    value = master[chunk, at:at + 16, yy * LANES:(yy + 1) * LANES]
+                    high = jnp.where(at_x == slot, pltpu.roll(value, (slot - 3) % LANES, 1) if slot < 3 else value, high)
                     low = jnp.where(at_x == slot, pltpu.roll(value, slot, 1) if slot else value, low)
             xs_out[0, step, chunk, off:off + 16] = high.astype(BF16)
             xs_out[1, step, chunk, off:off + 16] = low.astype(BF16)
@@ -292,46 +306,55 @@
     def table_of(step, chunk, yy):
         return coeff[pl.ds(pl.multiple_of((step * BLOCK + 2 * chunk + yy) * 8, 8), 8), :]
 
+    def outer_of(step, chunk, yy, rows):
+        factor = jnp.where(at_p == yy, table_of(step, chunk, yy)[5 + yy:6 + yy], 0.0)
+        return factor * pltpu.roll(rows.astype(F32), LANES - 4 if yy == 0 else 4, 1)
+
     def before_edges(step, chunk):
+        inner = jnp.dot(narrow[step, chunk], band[step, chunk], preferred_element_type=F32)
+        for yy in range(2):
+            lanes = slice(yy * LANES, (yy + 1) * LANES)
+            new = master[chunk, :, lanes] + inner[:, lanes]
+            if yy == 0 and chunk > 0:
+                new += outer_of(step, chunk, yy, narrow[step, chunk - 1, :, LANES:])
+            if yy == 1 and chunk < CHUNKS - 1:
+                new += outer_of(step, chunk, yy, narrow[step, chunk + 1, :, :LANES])
+            master[chunk, :, lanes] = new
+
+    def do_chunk(step, chunk):
+        both = has_side[0] & has_side[1]
+
+        @pl.when(both)
+        def _():
+            whole = xs_in.at[step, chunk]
+            pltpu.make_async_copy(whole, whole, x_recv.at[step, chunk]).wait()
+
+        @pl.when(jnp.logical_not(both))
+        def _():
+            one = xs_in.at[step, chunk, 0]
+            pltpu.make_async_copy(one, one, x_recv.at[step, chunk]).wait()
+
         if chunk == 0:
             y_copy(step, 0).wait_recv()
         if chunk == CHUNKS - 1:
             y_copy(step, 1).wait_recv()
-        inner = jnp.dot(narrow[step, chunk], band[step, chunk], preferred_element_type=F32)
-        for yy in range(2):
-            lanes = slice(yy * LANES, (yy + 1) * LANES)
-            if yy == 0:
-                outer = ys_in[step, 0] if chunk == 0 else narrow[step, chunk - 1, :, LANES:]
-            else:
-                outer = ys_in[step, 1] if chunk == CHUNKS - 1 else narrow[step, chunk + 1, :, :LANES]
-            k_outer = table_of(step, chunk, yy)[5 + yy:6 + yy]
-            master[chunk, :, lanes] += inner[:, lanes] + k_outer * outer.astype(F32)
-
-    def do_chunk(step, chunk):
-        both = has_side[0] & has_side[1]
-
-        @pl.when(both)
-        def _():
-            whole = xs_in.at[step, chunk]
-            pltpu.make_async_copy(whole, whole, x_recv.at[step, chunk]).wait()
-
-        @pl.when(jnp.logical_not(both))
-        def _():
-            one = xs_in.at[step, chunk, 0]
-            pltpu.make_async_copy(one, one, x_recv.at[step, chunk]).wait()
-
-        tables = [table_of(step, chunk, yy) for yy in range(2)]
-        for off in range(0, 64, 32):
+
+        for off in range(0, EDGE_ROWS, 32):
             halo_l = xs_in[step, chunk, 0, off:off + 32].astype(F32)
             halo_r = xs_in[step, chunk, 1, off:off + 32].astype(F32)
-            for q in range(4):
+            for q in range(2):
                 for yy in range(2):
                     slot = 2 * q + yy
-                    at = slice(off + q * 64, off + q * 64 + 32)
+                    at = slice(off + q * EDGE_ROWS, off + q * EDGE_ROWS + 32)
                     lanes = slice(yy * LANES, (yy + 1) * LANES)
                     from_l = pltpu.roll(halo_l, LANES - slot, 1) if slot else halo_l
-                    from_r = pltpu.roll(halo_r, 7 - slot, 1) if slot < 7 else halo_r
-                    new = master[chunk, at, lanes] + tables[yy][7:8] * jnp.where(at_x == 0, from_l, from_r)
+                    from_r = pltpu.roll(halo_r, 3 - slot, 1) if slot < 3 else halo_r
+                    factor = table_of(step, chunk, yy)[7:8]
+                    new = master[chunk, at, lanes] + factor * jnp.where(at_x == 0, from_l, from_r)
+                    if yy == 0 and chunk == 0:
+                        new += outer_of(step, chunk, yy, ys_in[step, 0, at])
+                    if yy == 1 and chunk == CHUNKS - 1:
+                        new += outer_of(step, chunk, yy, ys_in[step, 1, at])
                     master[chunk, at, lanes] = new
                     narrow[step + 1, chunk, at, lanes] = new.astype(BF16)
 
@@ -353,7 +376,7 @@
                 back_copy(chunk, k).start()
 
     def do_step(step, carry):
-        for chunk in (1, 2, 0, 3):
+        for chunk in ORDER:
             before_edges(step, chunk)
         for chunk in ORDER:
             do_chunk(step, chunk)
@@ -375,29 +398,32 @@
             drain(xs_out.at[side], x_send.at[side])
 
     drain(flux_out.at[pl.ds(0, GROUP - 1)], flux_send)
-    drain(sent.at[pl.ds(0, (GROUP - 1) * CHUNKS)], main_send)
+    drain(sent.at[pl.ds(0, GROUP - 1)], main_send)
     drain(ys_in, y_send)
     for chunk in ORDER:
         drain(back.at[chunk], back_recv.at[chunk])
-    drain(sent.at[pl.ds(0, (GROUP - 1) * CHUNKS)], back_send)
+    drain(sent.at[pl.ds(0, GROUP - 1)], back_send)
 
 
 def turn_back(back, out, part_in, wide, part_out, load, store):
     loads = [pltpu.make_async_copy(back.at[chunk], part_in.at[chunk], load.at[chunk]) for chunk in range(CHUNKS)]
     for copy in loads:
         copy.start()
+    at_p = lax.broadcasted_iota(jnp.int32, (1, LANES), 1) // 4 % 2
     for chunk in range(CHUNKS):
         loads[chunk].wait()
 
         def widen(of, carry, chunk=chunk):
             for yy in range(2):
-                y = of * BLOCK + 2 * chunk + yy
-                wide[pl.ds(pl.multiple_of(y * OWN, OWN), OWN), :] = part_in[
-                    chunk, of, :, yy * LANES:(yy + 1) * LANES
-                ].astype(F32)
+                lanes = slice(yy * LANES, (yy + 1) * LANES)
+                first = part_in[chunk, of, :, lanes].astype(F32)
+                second = part_in[chunk, of + 8, :, lanes].astype(F32)
+                at = pl.multiple_of((of * 16 + chunk * 4 + yy * 2) * OWN, 2 * OWN)
+                wide[pl.ds(at, OWN), :] = jnp.where(at_p == 0, first, pltpu.roll(second, 4, 1))
+                wide[pl.ds(at + OWN, OWN), :] = jnp.where(at_p == 0, pltpu.roll(first, LANES - 4, 1), second)
             return carry
 
-        lax.fori_loop(0, GROUP, widen, 0, unroll=4)
+        lax.fori_loop(0, 8, widen, 0, unroll=2)
     stores = []
     for part in range(4):
         for i in range(4):
@@ -424,7 +450,7 @@
             pltpu.VMEM((HID, SPEC), BF16),
             pltpu.VMEM((SPEC, HID), BF16),
             pltpu.VMEM((LANES * OWN, LANES), F32),
-            pltpu.VMEM((LANES // 2, OWN, PAIR), BF16),
+            pltpu.VMEM((GROUP, CHUNKS, OWN, PAIR), BF16),
             pltpu.VMEM((GROUP, BLOCK, LANES), BF16),
             pltpu.VMEM((GROUP, BLOCK, LANES), BF16),
             pltpu.VMEM((STEPS, BLOCK, LANES), F32),
@@ -433,8 +459,8 @@
             pltpu.VMEM((CHUNKS, SPEC, PAIR), F32),
             pltpu.VMEM((STEPS * 64, LANES), F32),
             pltpu.VMEM((STEPS, CHUNKS, PAIR, PAIR), BF16),
-            pltpu.VMEM((2, STEPS, CHUNKS, 64, LANES), BF16),
-            pltpu.VMEM((STEPS, CHUNKS, 2, 64, LANES), BF16),
+            pltpu.VMEM((2, STEPS, CHUNKS, EDGE_ROWS, LANES), BF16),
+            pltpu.VMEM((STEPS, CHUNKS, 2, EDGE_ROWS, LANES), BF16),
             pltpu.VMEM((STEPS, 2, SPEC, LANES), BF16),
             pltpu.VMEM((HID, PAIR), BF16),
             dma((7,)), dma(()), dma(()), dma((2,)), dma(()), dma((CHUNKS,)),

time: 50.1 us -> 46.9 us (0.936)
  Pallas kernels: 50 us -> 46.3 us
    pallas_call x1, Pallas kernels: 47.7 us -> 42.9 us  [per_device(): pl.pallas_call(transport, out_shape=jax.ShapeDtypeStruct((CHUNKS, GROUP,...]
    pallas_call x1, Pallas kernels: 2.29 us -> 3.35 us  [per_device(): pl.pallas_call(turn_back, out_shape=jax.ShapeDtypeStruct(tracers.shape, F...]
where the time goes in v4:
time: 46.9 us; the launch traced here: 46.3 us
  Pallas kernels  46.3 us (99%)
    pallas_call x1, Pallas kernels, per_device(): pl.pallas_call(transport, out_shape=jax.ShapeDtypeStruct((CHUNKS, GROUP,...  42.9 us
    pallas_call x1, Pallas kernels, per_device(): pl.pallas_call(turn_back, out_shape=jax.ShapeDtypeStruct(tracers.shape, F...  3.35 us

profile of v4, /device:TPU:1, one launch (start us, length us, event | category | flops | bytes accessed | tf_op | source)
XLA Modules:
  0.0 46.3 jit_solution(12086062682120758720)
XLA Ops:
  0.0 42.9 %transport.1.back = bf16[4,16,16,256]{3,2,1,0:T(8,128)(2,1)} custom-call(f32[16,16,8,128]{3,2,1,0:T(8,128)} %tracers_hbm.1, f32[4,3,1,8,128]{4,3,2,1,0:T(8,128)} %fluxes_hbm.1, bf16[512,256]{1,0:T(8,128)(2,1)} %weight_in_hbm.1, bf16[256,512]{1,0:T(8,128)(2,1)} %weight_out_hbm.1), custom_call_target="tpu_custom_call" | custom-call | tf_op jit(solution)/shard_map/transport/pallas_call | solution.py:442
  43.0 3.4 %turn_back.1 = f32[16,16,8,128]{3,2,1,0:T(8,128)} custom-call(bf16[4,16,16,256]{3,2,1,0:T(8,128)(2,1)} %transport.1.back), custom_call_target="tpu_custom_call" | custom-call | tf_op jit(solution)/shard_map/turn_back/pallas_call | solution.py:472

commit v5 on v4

--- a/solution.py
+++ b/solution.py
@@ -269,18 +269,19 @@
             y_copy(step, 1).start()
         if chunk == CHUNKS - 1:
             y_copy(step, 0).start()
-        for off in range(0, EDGE_ROWS, 16):
-            high = jnp.zeros((16, LANES), F32)
-            low = jnp.zeros((16, LANES), F32)
+        for off in range(0, EDGE_ROWS, 32):
+            high = low = None
             for q in range(2):
                 for yy in range(2):
                     slot = 2 * q + yy
                     at = q * EDGE_ROWS + off
-                    value = master[chunk, at:at + 16, yy * LANES:(yy + 1) * LANES]
-                    high = jnp.where(at_x == slot, pltpu.roll(value, (slot - 3) % LANES, 1) if slot < 3 else value, high)
-                    low = jnp.where(at_x == slot, pltpu.roll(value, slot, 1) if slot else value, low)
-            xs_out[0, step, chunk, off:off + 16] = high.astype(BF16)
-            xs_out[1, step, chunk, off:off + 16] = low.astype(BF16)
+                    value = narrow[step, chunk, at:at + 32, yy * LANES:(yy + 1) * LANES]
+                    up = pltpu.roll(value, (slot - 3) % LANES, 1) if slot < 3 else value
+                    down = pltpu.roll(value, slot, 1) if slot else value
+                    high = up if slot == 0 else jnp.where(at_x == slot, up, high)
+                    low = down if slot == 0 else jnp.where(at_x == slot, down, low)
+            xs_out[0, step, chunk, off:off + 32] = high
+            xs_out[1, step, chunk, off:off + 32] = low
         for side in range(2):
 
             @pl.when(has_side[1 - side])
@@ -340,8 +341,8 @@
             y_copy(step, 1).wait_recv()
 
         for off in range(0, EDGE_ROWS, 32):
-            halo_l = xs_in[step, chunk, 0, off:off + 32].astype(F32)
-            halo_r = xs_in[step, chunk, 1, off:off + 32].astype(F32)
+            halo_l = xs_in[step, chunk, 0, off:off + 32]
+            halo_r = xs_in[step, chunk, 1, off:off + 32]
             for q in range(2):
                 for yy in range(2):
                     slot = 2 * q + yy
@@ -350,7 +351,7 @@
                     from_l = pltpu.roll(halo_l, LANES - slot, 1) if slot else halo_l
                     from_r = pltpu.roll(halo_r, 3 - slot, 1) if slot < 3 else halo_r
                     factor = table_of(step, chunk, yy)[7:8]
-                    new = master[chunk, at, lanes] + factor * jnp.where(at_x == 0, from_l, from_r)
+                    new = master[chunk, at, lanes] + factor * jnp.where(at_x == 0, from_l, from_r).astype(F32)
                     if yy == 0 and chunk == 0:
                         new += outer_of(step, chunk, yy, ys_in[step, 0, at])
                     if yy == 1 and chunk == CHUNKS - 1:
@@ -423,7 +424,7 @@
                 wide[pl.ds(at + OWN, OWN), :] = jnp.where(at_p == 0, pltpu.roll(first, LANES - 4, 1), second)
             return carry
 
-        lax.fori_loop(0, 8, widen, 0, unroll=2)
+        lax.fori_loop(0, 8, widen, 0, unroll=8)
     stores = []
     for part in range(4):
         for i in range(4):

time: 46.9 us -> 46 us (0.981)
  Pallas kernels: 46.3 us -> 45.4 us
    pallas_call x1, Pallas kernels: 3.35 us -> 2.49 us  [per_device(): pl.pallas_call(turn_back, out_shape=jax.ShapeDtypeStruct(tracers.shape, F...]
where the time goes in v5:
time: 46 us; the launch traced here: 45.4 us
  Pallas kernels  45.4 us (99%)
    pallas_call x1, Pallas kernels, per_device(): pl.pallas_call(transport, out_shape=jax.ShapeDtypeStruct((CHUNKS, GROUP,...  42.9 us
    pallas_call x1, Pallas kernels, per_device(): pl.pallas_call(turn_back, out_shape=jax.ShapeDtypeStruct(tracers.shape, F...  2.49 us

profile of v5, /device:TPU:1, one launch (start us, length us, event | category | flops | bytes accessed | tf_op | source)
XLA Modules:
  0.0 45.4 jit_solution(15372363689367717907)
XLA Ops:
  0.0 42.9 %transport.1.back = bf16[4,16,16,256]{3,2,1,0:T(8,128)(2,1)} custom-call(f32[16,16,8,128]{3,2,1,0:T(8,128)} %tracers_hbm.1, f32[4,3,1,8,128]{4,3,2,1,0:T(8,128)} %fluxes_hbm.1, bf16[512,256]{1,0:T(8,128)(2,1)} %weight_in_hbm.1, bf16[256,512]{1,0:T(8,128)(2,1)} %weight_out_hbm.1), custom_call_target="tpu_custom_call" | custom-call | tf_op jit(solution)/shard_map/transport/pallas_call | solution.py:443
  42.9 2.5 %turn_back.1 = f32[16,16,8,128]{3,2,1,0:T(8,128)} custom-call(bf16[4,16,16,256]{3,2,1,0:T(8,128)(2,1)} %transport.1.back), custom_call_target="tpu_custom_call" | custom-call | tf_op jit(solution)/shard_map/turn_back/pallas_call | solution.py:473

commit v6 on v5

--- a/solution.py
+++ b/solution.py
@@ -17,6 +17,7 @@
 CHUNKS = 4
 EDGE_ROWS = 128
 ORDER = (0, 3, 1, 2)
+PLACE = (0, 2, 3, 1)
 PEERS = (8, 4, 12, 2, 9, 5, 13, 3, 10, 6, 14, 1, 11, 7, 15)
 F32 = jnp.float32
 BF16 = jnp.bfloat16
@@ -30,7 +31,7 @@
 def transport(
     tracers_hbm, fluxes_hbm, weight_in_hbm, weight_out_hbm, back,
     tracers, fluxes, weight_in, weight_out, turned, sent, flux_out, flux_in, beyond_out, beyond_in,
-    narrow, master, coeff, band, xs_out, xs_in, ys_in, hidden,
+    narrow, master, coeff, band, xs_out, xs_in, ys_out, ys_in, hidden,
     load, flux_send, flux_recv, beyond_sem, main_send, main_recv,
     x_send, x_recv, y_send, y_recv, back_send, back_recv,
 ):
@@ -121,7 +122,7 @@
                 at = pl.multiple_of((to * 16 + chunk * 4 + yy * 2) * OWN, 2 * OWN)
                 both = halves(turned[pl.ds(at, OWN), :], turned[pl.ds(at + OWN, OWN), :])
                 for of in range(2):
-                    sent[of * 8 + to, chunk, :, yy * LANES:(yy + 1) * LANES] = both[of].astype(BF16)
+                    sent[of * 8 + to, PLACE[chunk], :, yy * LANES:(yy + 1) * LANES] = both[of].astype(BF16)
         return carry
 
     lax.fori_loop(0, 8, narrowed, 0)
@@ -139,13 +140,13 @@
             device_id_type=MESH,
         )
 
-    def main_copy(chunk, k):
+    def main_copy(pair, k):
         peer = lax.rem(spec + k, GROUP)
         return pltpu.make_async_remote_copy(
-            src_ref=sent.at[block_of(peer), chunk],
-            dst_ref=narrow.at[0, chunk, mine],
+            src_ref=sent.at[block_of(peer), pl.ds(2 * pair, 2)],
+            dst_ref=narrow.at[0, pl.ds(2 * pair, 2), mine],
             send_sem=main_send,
-            recv_sem=main_recv.at[chunk],
+            recv_sem=main_recv.at[pair],
             device_id=(peer, tile),
             device_id_type=MESH,
         )
@@ -154,12 +155,11 @@
 
     for k in PEERS:
         flux_copy(k).start()
-    for chunk in ORDER:
-        pltpu.make_async_copy(
-            sent.at[block, chunk], narrow.at[0, chunk, mine], main_recv.at[chunk]
-        ).start()
+    for pair in range(2):
+        span = pl.ds(2 * pair, 2)
+        pltpu.make_async_copy(sent.at[block, span], narrow.at[0, span, mine], main_recv.at[pair]).start()
         for k in PEERS:
-            main_copy(chunk, k).start()
+            main_copy(pair, k).start()
 
     loads[5].wait()
     loads[6].wait()
@@ -192,6 +192,64 @@
         beyond_copy.start()
 
     others = [[field_of(step, field) for field in (1, 2, 3)] for step in range(STEPS)]
+
+    def x_copy(step, chunk, side):
+        return pltpu.make_async_remote_copy(
+            src_ref=xs_out.at[side, step, chunk],
+            dst_ref=xs_in.at[step, chunk, side],
+            send_sem=x_send.at[side],
+            recv_sem=x_recv.at[step, chunk],
+            device_id=side_devices[1 - side],
+            device_id_type=MESH,
+        )
+
+    def y_copy(step, side):
+        return pltpu.make_async_remote_copy(
+            src_ref=ys_out.at[step, side],
+            dst_ref=ys_in.at[step, side],
+            send_sem=y_send,
+            recv_sem=y_recv.at[step, side],
+            device_id=upper if side == 0 else lower,
+            device_id_type=MESH,
+        )
+
+    def publish_y(step, side):
+        chunk, at = (CHUNKS - 1, LANES) if side == 0 else (0, 0)
+        first = narrow[step, PLACE[chunk], :EDGE_ROWS, at:at + LANES]
+        second = narrow[step, PLACE[chunk], EDGE_ROWS:, at:at + LANES]
+        ys_out[step, side] = jnp.where(at_p == 1 - side, first, pltpu.roll(second, 4 if side else LANES - 4, 1))
+        y_copy(step, side).start()
+
+    def publish(step, chunk):
+        if chunk == 0:
+            publish_y(step, 1)
+        if chunk == CHUNKS - 1:
+            publish_y(step, 0)
+        for off in range(0, EDGE_ROWS, 32):
+            high = low = None
+            for q in range(2):
+                for yy in range(2):
+                    slot = 2 * q + yy
+                    at = q * EDGE_ROWS + off
+                    value = narrow[step, PLACE[chunk], at:at + 32, yy * LANES:(yy + 1) * LANES]
+                    up = pltpu.roll(value, (slot - 3) % LANES, 1) if slot < 3 else value
+                    down = pltpu.roll(value, slot, 1) if slot else value
+                    high = up if slot == 0 else jnp.where(at_x == slot, up, high)
+                    low = down if slot == 0 else jnp.where(at_x == slot, down, low)
+            xs_out[0, step, chunk, off:off + 32] = high
+            xs_out[1, step, chunk, off:off + 32] = low
+        for side in range(2):
+
+            @pl.when(has_side[1 - side])
+            def _(side=side):
+                x_copy(step, chunk, side).start()
+
+    for chunk in ORDER:
+        if PLACE[chunk] % 2 == 0:
+            whole = narrow.at[0, pl.ds(PLACE[chunk], 2)]
+            pltpu.make_async_copy(whole, whole, main_recv.at[PLACE[chunk] // 2]).wait()
+        master[chunk] = narrow[0, PLACE[chunk]].astype(F32)
+        publish(0, chunk)
 
     @pl.when(has_side[1])
     def _():
@@ -244,59 +302,10 @@
 
     lax.fori_loop(0, 8 * STEPS, bands, 0)
 
-    def x_copy(step, chunk, side):
-        return pltpu.make_async_remote_copy(
-            src_ref=xs_out.at[side, step, chunk],
-            dst_ref=xs_in.at[step, chunk, side],
-            send_sem=x_send.at[side],
-            recv_sem=x_recv.at[step, chunk],
-            device_id=side_devices[1 - side],
-            device_id_type=MESH,
-        )
-
-    def y_copy(step, side):
-        return pltpu.make_async_remote_copy(
-            src_ref=narrow.at[step, CHUNKS - 1 if side == 0 else 0, :, pl.ds(LANES if side == 0 else 0, LANES)],
-            dst_ref=ys_in.at[step, side],
-            send_sem=y_send,
-            recv_sem=y_recv.at[step, side],
-            device_id=upper if side == 0 else lower,
-            device_id_type=MESH,
-        )
-
-    def publish(step, chunk):
-        if chunk == 0:
-            y_copy(step, 1).start()
-        if chunk == CHUNKS - 1:
-            y_copy(step, 0).start()
-        for off in range(0, EDGE_ROWS, 32):
-            high = low = None
-            for q in range(2):
-                for yy in range(2):
-                    slot = 2 * q + yy
-                    at = q * EDGE_ROWS + off
-                    value = narrow[step, chunk, at:at + 32, yy * LANES:(yy + 1) * LANES]
-                    up = pltpu.roll(value, (slot - 3) % LANES, 1) if slot < 3 else value
-                    down = pltpu.roll(value, slot, 1) if slot else value
-                    high = up if slot == 0 else jnp.where(at_x == slot, up, high)
-                    low = down if slot == 0 else jnp.where(at_x == slot, down, low)
-            xs_out[0, step, chunk, off:off + 32] = high
-            xs_out[1, step, chunk, off:off + 32] = low
-        for side in range(2):
-
-            @pl.when(has_side[1 - side])
-            def _(side=side):
-                x_copy(step, chunk, side).start()
-
-    for chunk in ORDER:
-        pltpu.make_async_copy(narrow.at[0, chunk], narrow.at[0, chunk], main_recv.at[chunk]).wait()
-        master[chunk] = narrow[0, chunk].astype(F32)
-        publish(0, chunk)
-
     def back_copy(chunk, k):
         peer = lax.rem(spec + k, GROUP)
         return pltpu.make_async_remote_copy(
-            src_ref=narrow.at[STEPS, chunk, pl.ds(pl.multiple_of(peer * OWN, OWN), OWN)],
+            src_ref=narrow.at[STEPS, PLACE[chunk], pl.ds(pl.multiple_of(peer * OWN, OWN), OWN)],
             dst_ref=back.at[chunk, block],
             send_sem=back_send,
             recv_sem=back_recv.at[chunk],
@@ -307,19 +316,21 @@
     def table_of(step, chunk, yy):
         return coeff[pl.ds(pl.multiple_of((step * BLOCK + 2 * chunk + yy) * 8, 8), 8), :]
 
-    def outer_of(step, chunk, yy, rows):
+    def outer_of(step, chunk, yy, rows, in_place=False):
         factor = jnp.where(at_p == yy, table_of(step, chunk, yy)[5 + yy:6 + yy], 0.0)
-        return factor * pltpu.roll(rows.astype(F32), LANES - 4 if yy == 0 else 4, 1)
+        if not in_place:
+            rows = pltpu.roll(rows, LANES - 4 if yy == 0 else 4, 1)
+        return factor * rows.astype(F32)
 
     def before_edges(step, chunk):
-        inner = jnp.dot(narrow[step, chunk], band[step, chunk], preferred_element_type=F32)
+        inner = jnp.dot(narrow[step, PLACE[chunk]], band[step, chunk], preferred_element_type=F32)
         for yy in range(2):
             lanes = slice(yy * LANES, (yy + 1) * LANES)
             new = master[chunk, :, lanes] + inner[:, lanes]
             if yy == 0 and chunk > 0:
-                new += outer_of(step, chunk, yy, narrow[step, chunk - 1, :, LANES:])
+                new += outer_of(step, chunk, yy, narrow[step, PLACE[chunk - 1], :, LANES:])
             if yy == 1 and chunk < CHUNKS - 1:
-                new += outer_of(step, chunk, yy, narrow[step, chunk + 1, :, :LANES])
+                new += outer_of(step, chunk, yy, narrow[step, PLACE[chunk + 1], :, :LANES])
             master[chunk, :, lanes] = new
 
     def do_chunk(step, chunk):
@@ -353,18 +364,18 @@
                     factor = table_of(step, chunk, yy)[7:8]
                     new = master[chunk, at, lanes] + factor * jnp.where(at_x == 0, from_l, from_r).astype(F32)
                     if yy == 0 and chunk == 0:
-                        new += outer_of(step, chunk, yy, ys_in[step, 0, at])
+                        new += outer_of(step, chunk, yy, ys_in[step, 0, off:off + 32], q == 1)
                     if yy == 1 and chunk == CHUNKS - 1:
-                        new += outer_of(step, chunk, yy, ys_in[step, 1, at])
+                        new += outer_of(step, chunk, yy, ys_in[step, 1, off:off + 32], q == 1)
                     master[chunk, at, lanes] = new
-                    narrow[step + 1, chunk, at, lanes] = new.astype(BF16)
-
-        cells = narrow[step + 1, chunk]
+                    narrow[step + 1, PLACE[chunk], at, lanes] = new.astype(BF16)
+
+        cells = narrow[step + 1, PLACE[chunk]]
         pre = jnp.dot(weight_in[...], cells, preferred_element_type=F32)
         hidden[...] = (pre + pre * jnp.tanh(pre)).astype(BF16)
         after = master[chunk] + jnp.dot(weight_out[...], hidden[...], preferred_element_type=F32)
         master[chunk] = after
-        narrow[step + 1, chunk] = after.astype(BF16)
+        narrow[step + 1, PLACE[chunk]] = after.astype(BF16)
 
         @pl.when(step < STEPS - 1)
         def _():
@@ -372,7 +383,7 @@
 
         @pl.when(step == STEPS - 1)
         def _():
-            pltpu.make_async_copy(narrow.at[STEPS, chunk, mine], back.at[chunk, block], back_recv.at[chunk]).start()
+            pltpu.make_async_copy(narrow.at[STEPS, PLACE[chunk], mine], back.at[chunk, block], back_recv.at[chunk]).start()
             for k in PEERS:
                 back_copy(chunk, k).start()
 
@@ -462,7 +473,8 @@
             pltpu.VMEM((STEPS, CHUNKS, PAIR, PAIR), BF16),
             pltpu.VMEM((2, STEPS, CHUNKS, EDGE_ROWS, LANES), BF16),
             pltpu.VMEM((STEPS, CHUNKS, 2, EDGE_ROWS, LANES), BF16),
-            pltpu.VMEM((STEPS, 2, SPEC, LANES), BF16),
+            pltpu.VMEM((STEPS, 2, EDGE_ROWS, LANES), BF16),
+            pltpu.VMEM((STEPS, 2, EDGE_ROWS, LANES), BF16),
             pltpu.VMEM((HID, PAIR), BF16),
             dma((7,)), dma(()), dma(()), dma((2,)), dma(()), dma((CHUNKS,)),
             dma((2,)), dma((STEPS, CHUNKS)), dma(()), dma((STEPS, 2)), dma(()), dma((CHUNKS,)),

time: 46 us -> 43.4 us (0.943)
  Pallas kernels: 45.4 us -> 42.8 us
    pallas_call x1, Pallas kernels: 42.9 us -> 40.3 us  [per_device(): pl.pallas_call(transport, out_shape=jax.ShapeDtypeStruct((CHUNKS, GROUP,...]
where the time goes in v6:
time: 43.4 us; the launch traced here: 42.8 us
  Pallas kernels  42.8 us (99%)
    pallas_call x1, Pallas kernels, per_device(): pl.pallas_call(transport, out_shape=jax.ShapeDtypeStruct((CHUNKS, GROUP,...  40.3 us
    pallas_call x1, Pallas kernels, per_device(): pl.pallas_call(turn_back, out_shape=jax.ShapeDtypeStruct(tracers.shape, F...  2.49 us

profile of v6, /device:TPU:1, one launch (start us, length us, event | category | flops | bytes accessed | tf_op | source)
XLA Modules:
  0.0 42.8 jit_solution(11839573836540467920)
XLA Ops:
  0.0 40.3 %transport.1.back = bf16[4,16,16,256]{3,2,1,0:T(8,128)(2,1)} custom-call(f32[16,16,8,128]{3,2,1,0:T(8,128)} %tracers_hbm.1, f32[4,3,1,8,128]{4,3,2,1,0:T(8,128)} %fluxes_hbm.1, bf16[512,256]{1,0:T(8,128)(2,1)} %weight_in_hbm.1, bf16[256,512]{1,0:T(8,128)(2,1)} %weight_out_hbm.1), custom_call_target="tpu_custom_call" | custom-call | tf_op jit(solution)/shard_map/transport/pallas_call | solution.py:454
  40.4 2.5 %turn_back.1 = f32[16,16,8,128]{3,2,1,0:T(8,128)} custom-call(bf16[4,16,16,256]{3,2,1,0:T(8,128)(2,1)} %transport.1.back), custom_call_target="tpu_custom_call" | custom-call | tf_op jit(solution)/shard_map/turn_back/pallas_call | solution.py:485

commit v7 on v6

--- a/solution.py
+++ b/solution.py
@@ -16,8 +16,8 @@
 BLOCK = 8
 CHUNKS = 4
 EDGE_ROWS = 128
-ORDER = (0, 3, 1, 2)
-PLACE = (0, 2, 3, 1)
+ORDER = (1, 2, 0, 3)
+PLACE = (2, 0, 1, 3)
 PEERS = (8, 4, 12, 2, 9, 5, 13, 3, 10, 6, 14, 1, 11, 7, 15)
 F32 = jnp.float32
 BF16 = jnp.bfloat16
@@ -191,7 +191,6 @@
     def _():
         beyond_copy.start()
 
-    others = [[field_of(step, field) for field in (1, 2, 3)] for step in range(STEPS)]
 
     def x_copy(step, chunk, side):
         return pltpu.make_async_remote_copy(
@@ -250,6 +249,8 @@
             pltpu.make_async_copy(whole, whole, main_recv.at[PLACE[chunk] // 2]).wait()
         master[chunk] = narrow[0, PLACE[chunk]].astype(F32)
         publish(0, chunk)
+
+    others = [[field_of(step, field) for field in (1, 2, 3)] for step in range(STEPS)]
 
     @pl.when(has_side[1])
     def _():
@@ -437,11 +438,11 @@
 
         lax.fori_loop(0, 8, widen, 0, unroll=8)
     stores = []
-    for part in range(4):
-        for i in range(4):
-            own = part * 4 + i
+    for part in range(8):
+        for i in range(2):
+            own = part * 2 + i
             part_out[own] = wide[pl.ds(own, LANES, stride=OWN), :].T.reshape(16, 8, LANES)
-        span = pl.ds(4 * part, 4)
+        span = pl.ds(2 * part, 2)
         stores.append(pltpu.make_async_copy(part_out.at[span], out.at[span], store.at[part]))
         stores[-1].start()
     for copy in stores:
@@ -491,7 +492,7 @@
             pltpu.VMEM((CHUNKS, GROUP, OWN, PAIR), BF16),
             pltpu.VMEM((LANES * OWN, LANES), F32),
             pltpu.VMEM(tracers.shape, F32),
-            dma((CHUNKS,)), dma((4,)),
+            dma((CHUNKS,)), dma((8,)),
         ],
         compiler_params=pltpu.CompilerParams(vmem_limit_bytes=67043328),
         name="turn_back",

time: 43.4 us -> 43.1 us (level)
  no operation moved by 1% of the time
where the time goes in v7:
time: 43.1 us; the launch traced here: 42.8 us
  Pallas kernels  42.8 us (99%)
    pallas_call x1, Pallas kernels, per_device(): pl.pallas_call(transport, out_shape=jax.ShapeDtypeStruct((CHUNKS, GROUP,...  40.3 us
    pallas_call x1, Pallas kernels, per_device(): pl.pallas_call(turn_back, out_shape=jax.ShapeDtypeStruct(tracers.shape, F...  2.48 us

profile of v7, /device:TPU:1, one launch (start us, length us, event | category | flops | bytes accessed | tf_op | source)
XLA Modules:
  0.0 42.8 jit_solution(5625905986585649658)
XLA Ops:
  0.0 40.3 %transport.1.back = bf16[4,16,16,256]{3,2,1,0:T(8,128)(2,1)} custom-call(f32[16,16,8,128]{3,2,1,0:T(8,128)} %tracers_hbm.1, f32[4,3,1,8,128]{4,3,2,1,0:T(8,128)} %fluxes_hbm.1, bf16[512,256]{1,0:T(8,128)(2,1)} %weight_in_hbm.1, bf16[256,512]{1,0:T(8,128)(2,1)} %weight_out_hbm.1), custom_call_target="tpu_custom_call" | custom-call | tf_op jit(solution)/shard_map/transport/pallas_call | solution.py:455
  40.3 2.5 %turn_back.1 = f32[16,16,8,128]{3,2,1,0:T(8,128)} custom-call(bf16[4,16,16,256]{3,2,1,0:T(8,128)(2,1)} %transport.1.back), custom_call_target="tpu_custom_call" | custom-call | tf_op jit(solution)/shard_map/turn_back/pallas_call | solution.py:486
